TPU v7x, 32 devices: a whole 2x2x4 slice. The times are simulated.
32 devices in a mesh: dp: 8 (over y, x, core), seq: 4 (over z).
Axes of the slice: x: 2, y: 2, z: 4, core: 2. Of those that a mesh axis runs over, the one named last changes fastest.
Arguments:
- tokens: bfloat16 [96, 200, 512], P('dp', 'seq'), may hold values from -6 to 6
- ln1_gain: bfloat16 [512], P('dp'), may hold values from 0.5 to 1.5
- ln1_bias: bfloat16 [512], P('dp'), may hold values from -1 to 1
- w_qkv: bfloat16 [512, 1536], P('dp'), may hold values from -0.25 to 0.25
- w_out: bfloat16 [512, 512], P('dp'), may hold values from -1.75 to 1.75
- ln2_gain: bfloat16 [512], P('dp'), may hold values from 0.5 to 1.5
- ln2_bias: bfloat16 [512], P('dp'), may hold values from -1 to 1
- w_router: bfloat16 [512, 8], P('dp'), may hold values from -0.1875 to 0.1875
- expert_in: bfloat16 [8, 512, 2048], P('dp', None, 'seq'), may hold values from -0.25 to 0.25
- expert_out: bfloat16 [8, 2048, 512], P('dp', 'seq'), may hold values from -3 to 3
- routes: int32 [96, 200, 2], P('dp', 'seq'), may hold values from 0 to 7, all different within a row; in each aligned block of 50 rows (0 to 49, 50 to 99, ..., all dimensions but the last counted through in order) at most 14 rows name the same one
- targets: bfloat16 [96, 200, 512], P('dp', 'seq'), may hold values from -6 to 6
Outputs:
- mixed: bfloat16 [96, 200, 512], P('dp', 'seq')
- grad_tokens: float32 [96, 200, 512], P('dp', 'seq')
- grad_ln1_gain: float32 [512], P('dp')
- grad_ln1_bias: float32 [512], P('dp')
- grad_qkv: float32 [512, 1536], P('dp')
- grad_out: float32 [512, 512], P('dp')
- grad_ln2_gain: float32 [512], P('dp')
- grad_ln2_bias: float32 [512], P('dp')
- grad_router: float32 [512, 8], P('dp')
- grad_expert_in: float32 [8, 512, 2048], P('dp', None, 'seq')
- grad_expert_out: float32 [8, 2048, 512], P('dp', 'seq')
Inputs may be any that keep to these rules, and one draw needn't show every extreme that they name: `routes`: each slot names two different experts. In each aligned block of 50 rows (one image's slots on one device), no expert is named more than 14 times, and some expert reaches 14.
All inputs are finite; a program needn't handle non-finite values.
Results may differ from a plain program's by a relative error of at most 0.013.
Values may be sent and summed in bfloat16 or wider, within the bound.
A program may use at most 128 MiB of HBM per device.

v0:
```python
import functools

import jax
import jax.numpy as jnp
from jax import lax
from jax.experimental import pallas as pl
from jax.experimental.pallas import tpu as pltpu
from jax.sharding import PartitionSpec as P

H = 8
S = 200
VALID = 197


def layer_norm(values, gain_vec, bias_vec):
    centre = values - jnp.mean(values, axis=-1, keepdims=True)
    spread = jnp.mean(centre * centre, axis=-1, keepdims=True)
    return centre * lax.rsqrt(spread + 1e-06) * gain_vec + bias_vec


def regroup_heads(values):
    return lax.all_to_all(values, "seq", split_axis=3, concat_axis=1, tiled=True)


def regroup_slots(values):
    return lax.all_to_all(values, "seq", split_axis=1, concat_axis=3, tiled=True)


def send_experts(values):
    return lax.all_to_all(values, "dp", split_axis=0, concat_axis=1, tiled=True)


def send_tokens(values):
    return lax.all_to_all(values, "dp", split_axis=1, concat_axis=0, tiled=True)


def masked_scores(queries, keys_in, key_valid):
    scores = (
        jnp.einsum("bqhd,bkhd->bhqk", queries, keys_in, preferred_element_type=jnp.float32) * 0.125
    )
    return jnp.where(key_valid, scores, -1e30)


def attention_forward(queries, keys_in, values, key_valid):
    scores = masked_scores(queries, keys_in, key_valid)
    row_top = jnp.max(scores, axis=-1, keepdims=True)
    exponent = jnp.exp(scores - row_top)
    row_total = jnp.sum(exponent, axis=-1, keepdims=True)
    prob_rows = exponent / row_total
    log_total = row_top + jnp.log(row_total)
    attended = jnp.einsum(
        "bhqk,bkhd->bqhd",
        prob_rows.astype(jnp.bfloat16),
        values,
        preferred_element_type=jnp.float32,
    )
    return (attended.astype(jnp.bfloat16), log_total)


def attention_backward(queries, keys_in, values, log_total, grad_attended, key_valid):
    scores = masked_scores(queries, keys_in, key_valid)
    prob_rows = jnp.exp(scores - log_total)
    grad_values = jnp.einsum(
        "bhqk,bqhd->bkhd",
        prob_rows.astype(jnp.bfloat16),
        grad_attended,
        preferred_element_type=jnp.float32,
    )
    grad_probs = jnp.einsum(
        "bqhd,bkhd->bhqk", grad_attended, values, preferred_element_type=jnp.float32
    )
    inner_sum = jnp.sum(prob_rows * grad_probs, axis=-1, keepdims=True)
    grad_scores = (prob_rows * (grad_probs - inner_sum)).astype(jnp.bfloat16)
    grad_queries = (
        jnp.einsum("bhqk,bkhd->bqhd", grad_scores, keys_in, preferred_element_type=jnp.float32)
        * 0.125
    )
    grad_keys = (
        jnp.einsum("bhqk,bqhd->bkhd", grad_scores, queries, preferred_element_type=jnp.float32)
        * 0.125
    )
    return jnp.stack([grad_queries, grad_keys, grad_values], axis=2)


def pick_block(total_rows):
    for candidate in (1024, 768, 512, 384, 256):
        if total_rows % candidate == 0:
            return candidate
    return total_rows


def by_heads(
    tokens,
    ln1_gain,
    ln1_bias,
    w_qkv,
    w_out,
    ln2_gain,
    ln2_bias,
    w_router,
    expert_in,
    expert_out,
    routes,
    targets,
):
    image_count, slot_count, model_width = tokens.shape
    seq_devices = lax.axis_size("seq")
    row_count = image_count * slot_count
    expert_count = w_router.shape[1]
    local_experts = expert_in.shape[0]
    slot_limit = 2 * S // (seq_devices * expert_count) + 2
    head_size = model_width // H
    gathered = (
        lax.all_gather(ln1_gain, "dp", axis=0, tiled=True),
        lax.all_gather(ln1_bias, "dp", axis=0, tiled=True),
        lax.all_gather(w_qkv, "dp", axis=0, tiled=True),
        lax.all_gather(w_out, "dp", axis=0, tiled=True),
        lax.all_gather(ln2_gain, "dp", axis=0, tiled=True),
        lax.all_gather(ln2_bias, "dp", axis=0, tiled=True),
        lax.all_gather(w_router, "dp", axis=0, tiled=True),
    )
    gain_one = gathered[0].astype(jnp.float32)
    bias_one = gathered[1].astype(jnp.float32)
    qkv_weight = gathered[2]
    out_weight = gathered[3]
    gain_two = gathered[4].astype(jnp.float32)
    bias_two = gathered[5].astype(jnp.float32)
    router_weight = gathered[6]
    slot_start = lax.axis_index("seq") * slot_count
    valid_slot = slot_start + jnp.arange(slot_count) < VALID
    valid_rows = jnp.tile(valid_slot, image_count)
    key_valid = (jnp.arange(S) < VALID)[None, None, None, :]
    token_rows = tokens.reshape(row_count, model_width).astype(jnp.float32)
    normed_one, norm_one_back = jax.vjp(layer_norm, token_rows, gain_one, bias_one)
    normed_one_b = normed_one.astype(jnp.bfloat16)
    mixed_qkv = jnp.dot(normed_one_b, qkv_weight, preferred_element_type=jnp.float32).astype(
        jnp.bfloat16
    )
    qkv_heads = regroup_heads(mixed_qkv.reshape(image_count, slot_count, 3, H, head_size))
    queries = qkv_heads[:, :, 0]
    keys_in = qkv_heads[:, :, 1]
    values = qkv_heads[:, :, 2]
    attended, log_total = attention_forward(queries, keys_in, values, key_valid)
    attended_rows = regroup_slots(attended[:, :, None]).reshape(row_count, model_width)
    residual_two = token_rows + jnp.dot(
        attended_rows, out_weight, preferred_element_type=jnp.float32
    )
    normed_two, norm_two_back = jax.vjp(layer_norm, residual_two, gain_two, bias_two)
    normed_two_b = normed_two.astype(jnp.bfloat16)
    logits = jnp.dot(normed_two_b, router_weight, preferred_element_type=jnp.float32)
    route_rows = routes.reshape(row_count, 2)
    chosen = (route_rows[:, :, None] == jnp.arange(expert_count)[None, None, :]) & valid_rows[
        :, None, None
    ]
    chosen_f = chosen.astype(jnp.float32)

    def gate_pick(logit_rows):
        return jnp.sum(jax.nn.softmax(logit_rows, axis=-1)[:, None, :] * chosen_f, axis=-1)

    gate_values, gate_back = jax.vjp(gate_pick, logits)
    pick_count = chosen.astype(jnp.int32).reshape(image_count, slot_count * 2, expert_count)
    before = jnp.cumsum(pick_count, axis=1) - pick_count
    place_hit = (before[..., None] == jnp.arange(slot_limit)) & (pick_count[..., None] > 0)
    dispatch = place_hit.astype(jnp.bfloat16).reshape(
        image_count, slot_count, 2, expert_count, slot_limit
    )
    normed_img = normed_two_b.reshape(image_count, slot_count, model_width)
    sent_rows = jnp.einsum(
        "bskem,bsd->ebmd", dispatch, normed_img, preferred_element_type=jnp.float32
    ).astype(jnp.bfloat16)
    received = send_experts(sent_rows.reshape(expert_count, image_count * slot_limit, model_width))
    weights_in, weights_out = (
        lax.all_gather(expert_in, "seq", axis=2, tiled=True),
        lax.all_gather(expert_out, "seq", axis=1, tiled=True),
    )
    total_rows = received.shape[1]
    block_rows = pick_block(total_rows)
    block_count = total_rows // block_rows

    def expert_step(block_index, produced):
        row_piece = lax.dynamic_slice_in_dim(received, block_index * block_rows, block_rows, 1)
        hidden_pre = jnp.einsum(
            "erd,edf->erf", row_piece, weights_in, preferred_element_type=jnp.float32
        )
        activated = jax.nn.gelu(hidden_pre).astype(jnp.bfloat16)
        result = jnp.einsum(
            "erf,efd->erd", activated, weights_out, preferred_element_type=jnp.float32
        ).astype(jnp.bfloat16)
        return lax.dynamic_update_slice_in_dim(produced, result, block_index * block_rows, 1)

    produced = lax.fori_loop(
        0,
        block_count,
        expert_step,
        jnp.zeros((local_experts, total_rows, model_width), jnp.bfloat16),
    )
    returned = send_tokens(produced).reshape(expert_count, image_count, slot_limit, model_width)
    per_choice = jnp.einsum(
        "bskem,ebmd->bskd", dispatch, returned, preferred_element_type=jnp.float32
    ).reshape(row_count, 2, model_width)
    mixed_rows = (
        residual_two
        + gate_values[:, 0:1] * per_choice[:, 0]
        + gate_values[:, 1:2] * per_choice[:, 1]
    )
    target_rows = targets.reshape(row_count, model_width).astype(jnp.float32)
    grad_mixed = (mixed_rows - target_rows) * valid_rows[:, None].astype(jnp.float32)
    grad_gates = jnp.sum(grad_mixed[:, None, :] * per_choice, axis=-1)
    grad_choice = (
        (gate_values[:, :, None] * grad_mixed[:, None, :])
        .astype(jnp.bfloat16)
        .reshape(image_count, slot_count, 2, model_width)
    )
    grad_sent = jnp.einsum(
        "bskem,bskd->ebmd", dispatch, grad_choice, preferred_element_type=jnp.float32
    ).astype(jnp.bfloat16)
    grad_received = send_experts(
        grad_sent.reshape(expert_count, image_count * slot_limit, model_width)
    )
    back_in, back_out = (
        lax.all_gather(expert_in, "seq", axis=2, tiled=True),
        lax.all_gather(expert_out, "seq", axis=1, tiled=True),
    )

    def expert_back(block_index, loop_carry):
        grad_in_sum, grad_out_sum, grad_rows = loop_carry
        row_piece = lax.dynamic_slice_in_dim(received, block_index * block_rows, block_rows, 1)
        grad_piece = lax.dynamic_slice_in_dim(
            grad_received, block_index * block_rows, block_rows, 1
        )
        hidden_pre = jnp.einsum(
            "erd,edf->erf", row_piece, back_in, preferred_element_type=jnp.float32
        )
        activated, gelu_back = jax.vjp(jax.nn.gelu, hidden_pre)
        grad_act = jnp.einsum(
            "erd,efd->erf", grad_piece, back_out, preferred_element_type=jnp.float32
        )
        grad_pre = gelu_back(grad_act)[0].astype(jnp.bfloat16)
        grad_out_sum = grad_out_sum + jnp.einsum(
            "erf,erd->efd",
            activated.astype(jnp.bfloat16),
            grad_piece,
            preferred_element_type=jnp.float32,
        )
        grad_in_sum = grad_in_sum + jnp.einsum(
            "erd,erf->edf", row_piece, grad_pre, preferred_element_type=jnp.float32
        )
        rows_back = jnp.einsum(
            "erf,edf->erd", grad_pre, back_in, preferred_element_type=jnp.float32
        ).astype(jnp.bfloat16)
        grad_rows = lax.dynamic_update_slice_in_dim(
            grad_rows, rows_back, block_index * block_rows, 1
        )
        return (grad_in_sum, grad_out_sum, grad_rows)

    start_carry = (
        jnp.zeros(back_in.shape, jnp.float32),
        jnp.zeros(back_out.shape, jnp.float32),
        jnp.zeros((local_experts, total_rows, model_width), jnp.bfloat16),
    )
    grad_in_sum, grad_out_sum, grad_rows = lax.fori_loop(0, block_count, expert_back, start_carry)
    grad_returned = send_tokens(grad_rows).reshape(
        expert_count, image_count, slot_limit, model_width
    )
    grad_normed_two = jnp.einsum(
        "bskem,ebmd->bsd", dispatch, grad_returned, preferred_element_type=jnp.float32
    ).reshape(row_count, model_width)
    grad_logits = gate_back(grad_gates)[0].astype(jnp.bfloat16)
    grad_router = jnp.einsum(
        "rd,re->de", normed_two_b, grad_logits, preferred_element_type=jnp.float32
    )
    grad_normed_two = grad_normed_two + jnp.einsum(
        "re,de->rd", grad_logits, router_weight, preferred_element_type=jnp.float32
    )
    grad_res_two, grad_gain_two, grad_bias_two = norm_two_back(grad_normed_two)
    grad_residual = grad_mixed + grad_res_two
    grad_branch = grad_residual.astype(jnp.bfloat16)
    grad_out_weight = jnp.einsum(
        "rd,re->de", attended_rows, grad_branch, preferred_element_type=jnp.float32
    )
    grad_attended = jnp.einsum(
        "re,de->rd", grad_branch, out_weight, preferred_element_type=jnp.float32
    ).astype(jnp.bfloat16)
    grad_heads = regroup_heads(grad_attended.reshape(image_count, slot_count, 1, H, head_size))[
        :, :, 0
    ]
    grad_qkv_heads = attention_backward(
        queries, keys_in, values, log_total, grad_heads, key_valid
    ).astype(jnp.bfloat16)
    grad_qkv_rows = regroup_slots(grad_qkv_heads).reshape(row_count, 3 * model_width)
    grad_qkv_weight = jnp.einsum(
        "rd,rf->df", normed_one_b, grad_qkv_rows, preferred_element_type=jnp.float32
    )
    grad_normed_one = jnp.einsum(
        "rf,df->rd", grad_qkv_rows, qkv_weight, preferred_element_type=jnp.float32
    )
    grad_token_ln, grad_gain_one, grad_bias_one = norm_one_back(grad_normed_one)
    grad_tokens = grad_residual + grad_token_ln
    dense_grads = (
        grad_gain_one,
        grad_bias_one,
        grad_qkv_weight,
        grad_out_weight,
        grad_gain_two,
        grad_bias_two,
        grad_router,
    )
    dense_grads = (
        lax.psum(dense_grads[0].astype(jnp.bfloat16), "seq").astype(jnp.float32),
        lax.psum(dense_grads[1].astype(jnp.bfloat16), "seq").astype(jnp.float32),
        lax.psum(dense_grads[2].astype(jnp.bfloat16), "seq").astype(jnp.float32),
        lax.psum(dense_grads[3].astype(jnp.bfloat16), "seq").astype(jnp.float32),
        lax.psum(dense_grads[4].astype(jnp.bfloat16), "seq").astype(jnp.float32),
        lax.psum(dense_grads[5].astype(jnp.bfloat16), "seq").astype(jnp.float32),
        lax.psum(dense_grads[6].astype(jnp.bfloat16), "seq").astype(jnp.float32),
    )
    dense_grads = (
        lax.psum_scatter(
            dense_grads[0].astype(jnp.bfloat16), "dp", scatter_dimension=0, tiled=True
        ).astype(jnp.float32),
        lax.psum_scatter(
            dense_grads[1].astype(jnp.bfloat16), "dp", scatter_dimension=0, tiled=True
        ).astype(jnp.float32),
        lax.psum_scatter(
            dense_grads[2].astype(jnp.bfloat16), "dp", scatter_dimension=0, tiled=True
        ).astype(jnp.float32),
        lax.psum_scatter(
            dense_grads[3].astype(jnp.bfloat16), "dp", scatter_dimension=0, tiled=True
        ).astype(jnp.float32),
        lax.psum_scatter(
            dense_grads[4].astype(jnp.bfloat16), "dp", scatter_dimension=0, tiled=True
        ).astype(jnp.float32),
        lax.psum_scatter(
            dense_grads[5].astype(jnp.bfloat16), "dp", scatter_dimension=0, tiled=True
        ).astype(jnp.float32),
        lax.psum_scatter(
            dense_grads[6].astype(jnp.bfloat16), "dp", scatter_dimension=0, tiled=True
        ).astype(jnp.float32),
    )
    expert_in_grad, expert_out_grad = (
        lax.psum_scatter(
            grad_in_sum.astype(jnp.bfloat16), "seq", scatter_dimension=2, tiled=True
        ).astype(jnp.float32),
        lax.psum_scatter(
            grad_out_sum.astype(jnp.bfloat16), "seq", scatter_dimension=1, tiled=True
        ).astype(jnp.float32),
    )
    mixed = mixed_rows.astype(jnp.bfloat16).reshape(image_count, slot_count, model_width)
    return (
        mixed,
        grad_tokens.reshape(image_count, slot_count, model_width),
        dense_grads[0],
        dense_grads[1],
        dense_grads[2],
        dense_grads[3],
        dense_grads[4],
        dense_grads[5],
        dense_grads[6],
        expert_in_grad,
        expert_out_grad,
    )


BF = jnp.bfloat16
F32 = jnp.float32
MESH_ID = pl.DeviceIdType.MESH
NEG = -1e30
BP = 64
VMEM_LIMIT = 67000000
GELU_C = 0.7978845608028654
GELU_K = 0.044715


def nn(a, b):
    return lax.dot_general(a, b, (((1,), (0,)), ((), ())), preferred_element_type=F32)


def nt(a, b):
    return lax.dot_general(a, b, (((1,), (1,)), ((), ())), preferred_element_type=F32)


def tn(a, b):
    return lax.dot_general(a, b, (((0,), (0,)), ((), ())), preferred_element_type=F32)


def remote(src, dst, send_sem, recv_sem, dp, z):
    return pltpu.make_async_remote_copy(
        src_ref=src,
        dst_ref=dst,
        send_sem=send_sem,
        recv_sem=recv_sem,
        device_id=(dp, z),
        device_id_type=MESH_ID,
    )


def rows_of(index, size):
    return pl.ds(pl.multiple_of(index * size, size), size)


def norm_parts(x):
    centre = x - jnp.mean(x, axis=-1, keepdims=True)
    scale = lax.rsqrt(jnp.mean(centre * centre, axis=-1, keepdims=True) + 1e-06)
    return centre * scale, scale


def norm_back(grad_hat, hat, scale):
    return scale * (
        grad_hat
        - jnp.mean(grad_hat, axis=-1, keepdims=True)
        - hat * jnp.mean(grad_hat * hat, axis=-1, keepdims=True)
    )


def half_masks():
    lane = lax.broadcasted_iota(jnp.int32, (1, 128), 1)
    low = jnp.where(lane < 64, 1.0, 0.0).astype(BF)
    high = jnp.where(lane < 64, 0.0, 1.0).astype(BF)
    return (low, high)


def slot_ok(position, block):
    return (position % BP < block) & ((position // BP) * block + position % BP < VALID)


def block_kernel(
    dims,
    tok, tgt, rts, wq, wo, vec, win, wout,
    mixed, gtok, gqkv, gwo, gsmall, gin, gout,
    xin, rin, tin, vec_all, wq_all, wo_all, vsum, xpad, x2s, n2s, qkvs, outs, lses, gts, meta, metat,
    win_all, wout_all, recv, ret, acts, slopes, sbuf,
    mbuf, drows, dys, dlogs, dus, dret, dws, arrived,
    gacc, gvec, gbig, crecv, cvec, gsum, hrecv, hvec, zsend, zrecv, zall, zvec,
    loc_sem, tok_ss, tok_rs, rts_ss, rts_rs, tgt_ss, tgt_rs, den_ss, den_rs, fwd_ss, win_ss, win_rs, wout_ss, wout_rs,
    row_ss, row_rs, u_ss, u_rs, du_ss, du_rs, dn_ss, dn_rs, mix_ss, mix_rs, gt_ss, gt_rs,
    r_ss, r_rs, c_ss, c_rs, cv_ss, cv_rs, h_ss, h_rs, hv_ss, hv_rs, za_ss, za_rs, zb_ss, zb_rs, zv_ss, zv_rs,
):
    n_dp, n_z, im, block, cap, er = dims
    me, z = lax.axis_index("dp"), lax.axis_index("seq")
    sp = n_z * BP
    nr = n_dp * er
    two = 2 * er
    half = n_dp // 2
    last = n_z - 1
    core, chip = lax.rem(me, 2), me // 2
    partner = chip * 2 + 1 - core

    barrier = pltpu.get_barrier_semaphore()
    for k in range(1, n_dp):
        pl.semaphore_signal(barrier, inc=1, device_id=(lax.rem(me + k, n_dp), z), device_id_type=MESH_ID)
    for k in range(1, n_z):
        pl.semaphore_signal(barrier, inc=1, device_id=(me, lax.rem(z + k, n_z)), device_id_type=MESH_ID)
    own_copies = [
        pltpu.make_async_copy(tok.at[pl.ds(z * im, im)], xin.at[z], loc_sem.at[0]),
        pltpu.make_async_copy(rts.at[pl.ds(z * im, im)], rin.at[z], loc_sem.at[1]),
        pltpu.make_async_copy(tgt.at[pl.ds(z * im, im)], tin.at[z], loc_sem.at[2]),
        pltpu.make_async_copy(win, win_all.at[z], loc_sem.at[3]),
        pltpu.make_async_copy(wout, wout_all.at[z], loc_sem.at[4]),
        pltpu.make_async_copy(wq, wq_all.at[rows_of(me, 64)], loc_sem.at[5]),
        pltpu.make_async_copy(wo, wo_all.at[rows_of(me, 64)], loc_sem.at[6]),
        pltpu.make_async_copy(vec, vec_all.at[me], loc_sem.at[7]),
    ]
    for copy in own_copies:
        copy.start()
    xpad[...] = jnp.zeros_like(xpad)
    gacc[...] = jnp.zeros_like(gacc)
    gvec[...] = jnp.zeros_like(gvec)
    pl.semaphore_wait(barrier, n_dp + n_z - 2)

    def z_start(source, target, send_sem, recv_sem):
        for k in range(1, n_z):
            peer = lax.rem(z + k, n_z)
            remote(source(peer), target(z), send_sem.at[k], recv_sem.at[z], me, peer).start()

    def z_arrive(target, recv_sem):
        for k in range(1, n_z):
            origin = lax.rem(z + k, n_z)
            remote(target(origin), target(origin), loc_sem.at[8], recv_sem.at[origin], me, z).wait_recv()

    def z_sent(source, send_sem):
        for k in range(1, n_z):
            remote(source(0), source(0), send_sem.at[k], loc_sem.at[8], me, z).wait_send()

    tok_of = lambda peer: tok.at[pl.ds(peer * im, im)]
    rts_of = lambda peer: rts.at[pl.ds(peer * im, im)]
    tgt_of = lambda peer: tgt.at[pl.ds(peer * im, im)]
    z_start(tok_of, lambda i: xin.at[i], tok_ss, tok_rs)
    z_start(rts_of, lambda i: rin.at[i], rts_ss, rts_rs)

    def dense_slot(array, index):
        if array == 0:
            return wq_all.at[rows_of(index, 64)]
        if array == 1:
            return wo_all.at[rows_of(index, 64)]
        return vec_all.at[index]

    dense_in = (wq, wo, vec)
    for array in range(3):
        for k in range(1, half):
            peer = lax.rem(chip + k, half) * 2 + core
            remote(
                dense_in[array], dense_slot(array, me), den_ss.at[array, k], den_rs.at[array, me], peer, z
            ).start()
        remote(
            dense_in[array], dense_slot(array, me), den_ss.at[array, 0], den_rs.at[array, me], partner, z
        ).start()

    experts = ((win, win_all, win_ss, win_rs), (wout, wout_all, wout_ss, wout_rs))
    inner = (z == 1) | (z == last - 1)
    far_end = jnp.where(z == 1, last, 0)

    def weight_send(array, kind, there, peer):
        source, full, send_sem, recv_sem = experts[array]

        @pl.when(there)
        def _():
            remote(source, full.at[z], send_sem.at[kind], recv_sem.at[z], me, peer).start()

    for array in range(2):
        weight_send(array, 0, z >= 0, jnp.where(z < 2, z + 2, z - 2))
    for array in range(2):
        weight_send(array, 1, z < last, z + 1)
        weight_send(array, 2, z > 0, z - 1)

    def weight_wait(array, slot):
        source, full, send_sem, recv_sem = experts[array]
        at = full.at[slot]
        remote(at, at, send_sem.at[0], recv_sem.at[slot], me, z).wait_recv()

    def weight_forward(array):
        source, full, send_sem, recv_sem = experts[array]

        @pl.when(inner)
        def _():
            weight_wait(array, far_end)
            at = full.at[far_end]
            remote(at, at, send_sem.at[3], recv_sem.at[far_end], me, last - far_end).start()

    def weights_sent():
        for kind, there in ((0, z >= 0), (1, z < last), (2, z > 0), (3, inner)):

            @pl.when(there)
            def _():
                for source, full, send_sem, recv_sem in experts:
                    remote(full.at[0], full.at[0], send_sem.at[kind], recv_sem.at[0], me, z).wait_send()

    for k in range(1, half):
        origin = lax.rem(chip + k, half) * 2 + core
        for array in range(3):
            slot = dense_slot(array, origin)
            remote(slot, slot, den_ss.at[array, 0], den_rs.at[array, origin], me, z).wait_recv()
            remote(slot, slot, fwd_ss.at[array, k], den_rs.at[array, origin], partner, z).start()
    for k in range(half):
        origin = lax.rem(chip + k, half) * 2 + 1 - core
        for array in range(3):
            slot = dense_slot(array, origin)
            remote(slot, slot, den_ss.at[array, 0], den_rs.at[array, origin], me, z).wait_recv()
    for copy in own_copies:
        copy.wait()
    total = vec_all[0].astype(F32)
    for k in range(1, n_dp):
        total = total + vec_all[k].astype(F32)
    vsum[...] = total
    z_arrive(lambda i: xin.at[i], tok_rs)
    z_arrive(lambda i: rin.at[i], rts_rs)

    masks = half_masks()
    keys_ok = slot_ok(lax.broadcasted_iota(jnp.int32, (1, sp), 1), block)
    rows_ok = slot_ok(lax.broadcasted_iota(jnp.int32, (sp, 1), 0), block)
    gain_one, bias_one = vsum[0:1, :], vsum[1:2, :]
    gain_two, bias_two = vsum[2:3, :], vsum[3:4, :]
    router_t = vsum[8:16, :].astype(BF)
    lane_id = lax.broadcasted_iota(jnp.int32, (sp, 128), 1)
    lane_low = lane_id < 64

    def front(i, carry):
        before = lax.broadcasted_iota(jnp.int32, (sp, sp), 0)
        after = lax.broadcasted_iota(jnp.int32, (sp, sp), 1)
        prefix = jnp.where((before < after) & (before // BP == after // BP), 1.0, 0.0).astype(BF)
        expert_id = lax.broadcasted_iota(jnp.int32, (8, sp), 0)
        slot_lane = lax.broadcasted_iota(jnp.int32, (8, sp), 1)
        for b in range(n_z):
            xpad[i, b * BP : b * BP + block, :] = xin[b, i]
        x = xpad[i].astype(F32)
        hat, _ = norm_parts(x)
        normed = (hat * gain_one + bias_one).astype(BF)
        qkvs[i] = nn(normed, wq_all[...]).astype(BF)
        lse_all = jnp.zeros((sp, 128), F32)
        for pair in range(4):
            q2 = qkvs[i, :, pair * 128 : pair * 128 + 128]
            k2 = qkvs[i, :, 512 + pair * 128 : 512 + pair * 128 + 128]
            v2 = qkvs[i, :, 1024 + pair * 128 : 1024 + pair * 128 + 128]
            parts = []
            for side in range(2):
                scores = nt(q2 * masks[side], k2) * 0.125
                scores = jnp.where(keys_ok, scores, NEG)
                top = jnp.max(scores, axis=-1, keepdims=True)
                exponent = jnp.exp(scores - top)
                whole = jnp.sum(exponent, axis=-1, keepdims=True)
                lse_all = jnp.where(lane_id == pair * 2 + side, top + jnp.log(whole), lse_all)
                parts.append(nn((exponent / whole).astype(BF), v2))
            outs[i, :, pair * 128 : pair * 128 + 128] = jnp.where(lane_low, parts[0], parts[1]).astype(BF)
        lses[i] = lse_all
        x2 = x + nn(outs[i], wo_all[...])
        x2s[i] = x2
        hat2, _ = norm_parts(x2)
        n2 = (hat2 * gain_two + bias_two).astype(BF)
        n2s[i] = n2
        logits = nt(router_t, n2)
        raised = jnp.exp(logits - jnp.max(logits, axis=0, keepdims=True))
        share = raised / jnp.sum(raised, axis=0, keepdims=True)
        gts[i] = share
        wide = jnp.concatenate([rin[0, i] + rin[1, i], rin[2, i] + rin[3, i]], axis=1)
        hits = [(expert_id + 1) == wide[j : j + 1, :] for j in range(2)]
        any_hit = jnp.where(hits[0] | hits[1], 1.0, 0.0)
        place = nn(any_hit.astype(BF), prefix)
        base = place + (expert_id * er + (slot_lane // BP) * cap + i * (n_z * cap) + 1).astype(F32)
        lines = [jnp.sum(jnp.where(hit, base, 0.0), axis=0, keepdims=True) - 1.0 for hit in hits]
        lines += [jnp.sum(jnp.where(hit, share, 0.0), axis=0, keepdims=True) for hit in hits]
        table = jnp.concatenate(lines + [jnp.zeros((124, sp), F32)], axis=0)
        meta[i] = table[0:8]
        metat[i] = jnp.transpose(table)
        return carry

    lax.fori_loop(0, im, front, 0)

    row_id = lax.broadcasted_iota(jnp.int32, (er, sp), 0)

    def to_experts(product, target, send_sem, recv_sem):
        def step(s, carry):
            j, c = lax.rem(s // 2 + 1, half), lax.rem(s, 2)
            index = 2 * j + c
            peer = lax.rem(chip + j, half) * 2 + lax.rem(core + c, 2)
            sbuf[index] = product(peer).astype(BF)

            @pl.when(index > 0)
            def _():
                remote(
                    sbuf.at[index], target.at[rows_of(me, er)], send_sem.at[index], recv_sem.at[me], peer, z
                ).start()

            @pl.when(index == 0)
            def _():
                target[rows_of(me, er)] = sbuf[index]

            return carry

        lax.fori_loop(0, n_dp, step, 0)

    def to_tokens(product, target, send_sem, recv_sem):
        def step(s, carry):
            j = lax.rem(s + 1, half)
            part = lax.rem(chip + j, half)
            out = product(part).astype(BF)
            sbuf[2 * j] = out[0:er]
            sbuf[2 * j + 1] = out[er:two]

            @pl.when(j > 0)
            def _():
                for c in range(2):
                    remote(
                        sbuf.at[2 * j + c],
                        target.at[rows_of(me, er)],
                        send_sem.at[2 * j + c],
                        recv_sem.at[me],
                        part * 2 + c,
                        z,
                    ).start()

            @pl.when(j == 0)
            def _():
                target[rows_of(me, er)] = sbuf[core]
                remote(
                    sbuf.at[1 - core], target.at[rows_of(me, er)], send_sem.at[1], recv_sem.at[me], partner, z
                ).start()

            return carry

        lax.fori_loop(0, half, step, 0)

    def dp_arrive(target, recv_sem):
        for k in range(1, n_dp):
            origin = lax.rem(me + k, n_dp)
            spot = target.at[rows_of(origin, er)]
            remote(spot, spot, loc_sem.at[8], recv_sem.at[origin], me, z).wait_recv()

    def dp_sent(send_sem):
        for k in range(1, n_dp):
            remote(sbuf.at[0], sbuf.at[0], send_sem.at[k], loc_sem.at[8], me, z).wait_send()

    def tokens_for(peer):
        want = (row_id + peer * er).astype(F32)
        total = jnp.zeros((er, 512), F32)
        for i in range(im):
            pick = (want == meta[i, 0:1, :]) | (want == meta[i, 1:2, :])
            total = total + nn(jnp.where(pick, 1.0, 0.0).astype(BF), n2s[i])
        return total

    to_experts(tokens_for, recv, row_ss, row_rs)

    def hidden(shard):
        def part_step(part, carry):
            at = rows_of(part, two)
            x = recv[at]
            for side in range(2):
                pre = nn(x, win_all[shard, :, side * 256 : side * 256 + 256])
                square = pre * pre
                tanh = jnp.tanh(pre * (GELU_C + (GELU_C * GELU_K) * square))
                gate = 0.5 + 0.5 * tanh
                acts[shard, at, side * 256 : side * 256 + 256] = (pre * gate).astype(BF)
                slope = gate + pre * (0.5 - 0.5 * tanh * tanh) * (GELU_C + (3.0 * GELU_C * GELU_K) * square)
                slopes[shard, at, side * 256 : side * 256 + 256] = slope.astype(BF)
            return carry

        lax.fori_loop(0, n_dp // 2, part_step, 0)

    def hidden_step(s, carry):
        second = jnp.where(z == 0, 2, jnp.where(z == last, 1, last - far_end))
        shard = jnp.where(
            s == 0,
            z,
            jnp.where(
                s == 1,
                jnp.where(inner, far_end, jnp.where(z == 0, 1, last - 1)),
                jnp.where(s == 2, second, last - z),
            ),
        )

        @pl.when(inner & (s == 1))
        def _():
            weight_forward(1)

        @pl.when((s > 1) | ((s == 1) & jnp.logical_not(inner)))
        def _():
            weight_wait(0, shard)

        hidden(shard)
        return carry

    weight_forward(0)
    dp_arrive(recv, row_rs)
    dp_sent(row_ss)
    lax.fori_loop(0, n_z, hidden_step, 0)
    for slot in range(n_z):

        @pl.when((z != slot) & jnp.logical_not(inner & (far_end == slot)))
        def _():
            weight_wait(1, slot)

    z_start(tgt_of, lambda i: tin.at[i], tgt_ss, tgt_rs)

    def results_for(part):
        total = jnp.zeros((two, 512), F32)
        for shard in range(n_z):
            total = total + nn(acts[shard, rows_of(part, two)], wout_all[shard])
        return total

    to_tokens(results_for, ret, u_ss, u_rs)

    z_arrive(lambda i: tin.at[i], tgt_rs)
    for b in range(n_z):
        for i in range(im):
            dys[i, b * BP : b * BP + block, :] = tin[b, i].astype(F32)
    dp_arrive(ret, u_rs)

    def mix(i, carry):
        line = lax.broadcasted_iota(jnp.int32, (sp, nr), 1).astype(F32)
        cols = metat[i]
        picked = []
        for j in range(2):
            pick = jnp.where(line == cols[:, j : j + 1], 1.0, 0.0).astype(BF)
            picked.append(nn(pick, ret[...]))
        mix = x2s[i] + cols[:, 2:3] * picked[0] + cols[:, 3:4] * picked[1]
        mix_b = mix.astype(BF)
        for b in range(n_z):
            mbuf[b, i] = mix_b[b * BP : b * BP + block]
        dy = jnp.where(rows_ok, mix - dys[i], 0.0)
        dys[i] = dy
        dus[0, i] = (cols[:, 2:3] * dy).astype(BF)
        dus[1, i] = (cols[:, 3:4] * dy).astype(BF)
        dlogs[i] = jnp.where(
            lane_id == 0, jnp.sum(dy * picked[0], axis=-1, keepdims=True), 0.0
        ) + jnp.where(lane_id == 1, jnp.sum(dy * picked[1], axis=-1, keepdims=True), 0.0)
        return carry

    lax.fori_loop(0, im, mix, 0)
    dp_sent(u_ss)

    def gradients_for(peer):
        want = (row_id + peer * er).astype(F32)
        total = jnp.zeros((er, 512), F32)
        for i in range(im):
            for j in range(2):
                pick = jnp.where(want == meta[i, j : j + 1, :], 1.0, 0.0).astype(BF)
                total = total + nn(pick, dus[j, i])
        return total

    to_experts(gradients_for, drows, du_ss, du_rs)
    z_start(lambda peer: mbuf.at[peer], lambda i: mixed.at[pl.ds(i * im, im)], mix_ss, mix_rs)
    own_mixed = pltpu.make_async_copy(mbuf.at[z], mixed.at[pl.ds(z * im, im)], loc_sem.at[0])
    own_mixed.start()
    expert_row = lax.broadcasted_iota(jnp.int32, (8, sp), 0).astype(F32)
    for i in range(im):
        flat = jnp.transpose(dlogs[i])
        share = gts[i]
        grad = jnp.zeros((8, sp), F32)
        for j in range(2):
            at = meta[i, j : j + 1, :]
            inside = (at >= expert_row * er) & (at < expert_row * er + er)
            grad = grad + jnp.where(inside, flat[j : j + 1, :], 0.0)
        dlog = share * (grad - jnp.sum(share * grad, axis=0, keepdims=True))
        gts[i] = dlog
        gvec[8:16, :] += nn(dlog.astype(BF), n2s[i])
    dp_arrive(drows, du_rs)
    dp_sent(du_ss)

    def reduce_start(target, piece):
        held = inner & (target == far_end)
        via = ((z == 0) & (target == last)) | ((z == last) & (target == 0))
        peer = jnp.where(via, jnp.where(z == 0, 1, last - 1), target)

        @pl.when((target != z) & jnp.logical_not(held))
        def _():
            slot = jnp.where(via, peer, z)
            remote(
                dws.at[target, piece], arrived.at[slot, piece], r_ss.at[target, piece], r_rs.at[slot, piece], me, peer
            ).start()

    def reduce_forward(piece):
        @pl.when(inner)
        def _():
            here = arrived.at[z, piece]
            remote(here, here, r_ss.at[far_end, piece], r_rs.at[z, piece], me, z).wait_recv()

            def add(c, carry):
                at = rows_of(c, 128)
                dws[far_end, piece, at] = (
                    dws[far_end, piece, at].astype(F32) + arrived[z, piece, at].astype(F32)
                ).astype(BF)
                return carry

            lax.fori_loop(0, 4, add, 0)
            remote(
                dws.at[far_end, piece], here, r_ss.at[far_end, piece], r_rs.at[z, piece], me, far_end
            ).start()

    def owner(s):
        return jnp.where(z < n_z // 2, lax.rem(z + 2 * n_z - 1 - s, n_z), lax.rem(z + 1 + s, n_z))

    def out_grads(s, carry):
        target = owner(s)
        dws[target, 0] = tn(acts[target], drows[...]).astype(BF)
        reduce_start(target, 0)
        return carry

    def in_grads(s, carry):
        target = owner(s)
        dws[target, 1] = tn(recv[...], slopes[target]).astype(BF)
        reduce_start(target, 1)
        return carry

    lax.fori_loop(0, n_z, out_grads, 0)

    def input_grads_for(part):
        at = rows_of(part, two)
        du = drows[at]
        total = jnp.zeros((two, 512), F32)
        for shard in range(n_z):
            dpre = (nt(du, wout_all[shard]) * slopes[shard, at].astype(F32)).astype(BF)
            slopes[shard, at] = dpre
            total = total + nt(dpre, win_all[shard])
        return total

    to_tokens(input_grads_for, dret, dn_ss, dn_rs)
    lax.fori_loop(0, n_z, in_grads, 0)
    own_mixed.wait()
    z_sent(lambda peer: mbuf.at[peer], mix_ss)
    dp_arrive(dret, dn_rs)
    reduce_forward(0)

    def back(i, carry):
        line = lax.broadcasted_iota(jnp.int32, (sp, nr), 1).astype(F32)
        cols = metat[i]
        pick = jnp.where((line == cols[:, 0:1]) | (line == cols[:, 1:2]), 1.0, 0.0).astype(BF)
        dn2 = nn(pick, dret[...]) + tn(gts[i].astype(BF), router_t)
        hat2, scale2 = norm_parts(x2s[i])
        gvec[2:3, :] += jnp.sum(dn2 * hat2, axis=0, keepdims=True)
        gvec[3:4, :] += jnp.sum(dn2, axis=0, keepdims=True)
        dx2 = dys[i] + norm_back(dn2 * gain_two, hat2, scale2)
        da = dx2.astype(BF)
        gacc[:, 1536:2048] += tn(outs[i], da)
        do = nt(da, wo_all[...]).astype(BF)
        hat1, scale1 = norm_parts(xpad[i].astype(F32))
        n1 = (hat1 * gain_one + bias_one).astype(BF)
        dn1 = jnp.zeros((sp, 512), F32)
        for pair in range(4):
            at = pair * 128
            q2 = qkvs[i, :, at : at + 128]
            k2 = qkvs[i, :, 512 + at : 512 + at + 128]
            v2 = qkvs[i, :, 1024 + at : 1024 + at + 128]
            do2 = do[:, at : at + 128]
            grads = ([], [], [])
            for side in range(2):
                head = pair * 2 + side
                scores = nt(q2 * masks[side], k2) * 0.125
                scores = jnp.where(keys_ok, scores, NEG)
                prob = jnp.exp(scores - lses[i, :, head : head + 1])
                dprob = nt(do2 * masks[side], v2)
                inner = jnp.sum(prob * dprob, axis=-1, keepdims=True)
                ds = (prob * (dprob - inner)).astype(BF)
                grads[0].append(nn(ds, k2))
                grads[1].append(tn(ds, q2))
                grads[2].append(tn(prob.astype(BF), do2))
            for part in range(3):
                grad = jnp.where(lane_low, grads[part][0], grads[part][1])
                if part < 2:
                    grad = grad * 0.125
                grad = grad.astype(BF)
                col = part * 512 + at
                gacc[:, col : col + 128] += tn(n1, grad)
                dn1 = dn1 + nt(grad, wq_all[:, col : col + 128])
        gvec[0:1, :] += jnp.sum(dn1 * hat1, axis=0, keepdims=True)
        gvec[1:2, :] += jnp.sum(dn1, axis=0, keepdims=True)
        dx = (dx2 + norm_back(dn1 * gain_one, hat1, scale1)).astype(BF)
        for b in range(n_z):
            mbuf[b, i] = dx[b * BP : b * BP + block]
        return carry

    lax.fori_loop(0, im, back, 0)
    z_start(lambda peer: mbuf.at[peer], lambda i: gtok.at[pl.ds(i * im, im)], gt_ss, gt_rs)
    own_gtok = pltpu.make_async_copy(mbuf.at[z], gtok.at[pl.ds(z * im, im)], loc_sem.at[1])
    own_gtok.start()

    gbig[...] = gacc[...].astype(BF)
    for q in range(half):
        remote(
            gbig.at[rows_of(2 * q + 1 - core, 64)], crecv.at[q], c_ss.at[q], c_rs.at[q], partner, z
        ).start()
    remote(gvec, cvec, cv_ss.at[0], cv_rs.at[0], partner, z).start()
    for q in range(half):
        remote(crecv.at[q], crecv.at[q], c_ss.at[q], c_rs.at[q], me, z).wait_recv()
    for k in range(1, half):
        q = lax.rem(chip + k, half)
        gsum[q] = (gacc[rows_of(2 * q + core, 64)] + crecv[q].astype(F32)).astype(BF)
        remote(gsum.at[q], hrecv.at[chip], h_ss.at[k], h_rs.at[chip], q * 2 + core, z).start()
    remote(cvec, cvec, cv_ss.at[0], cv_rs.at[0], me, z).wait_recv()
    hvec[chip] = gvec[...] + cvec[...]
    for k in range(1, half):
        q = lax.rem(chip + k, half)
        remote(hvec.at[chip], hvec.at[chip], hv_ss.at[k], hv_rs.at[chip], q * 2 + core, z).start()
    reduce_forward(1)
    dense = gacc[rows_of(me, 64)] + crecv[chip].astype(F32)
    for k in range(1, half):
        q = lax.rem(chip + k, half)
        remote(hrecv.at[q], hrecv.at[q], h_ss.at[0], h_rs.at[q], me, z).wait_recv()
        dense = dense + hrecv[q].astype(F32)
    for peer in range(n_z):
        zsend[peer] = dense[peer * 16 : peer * 16 + 16].astype(BF)
    z_start(lambda peer: zsend.at[peer], lambda i: zrecv.at[i], za_ss, za_rs)
    for k in range(1, half):
        q = lax.rem(chip + k, half)
        remote(hvec.at[q], hvec.at[q], hv_ss.at[0], hv_rs.at[q], me, z).wait_recv()
    zvec[z] = hvec[0] + hvec[1] + hvec[2] + hvec[3]
    z_start(lambda peer: zvec.at[z], lambda i: zvec.at[i], zv_ss, zv_rs)
    zrecv[z] = zsend[z]
    z_arrive(lambda i: zrecv.at[i], za_rs)
    total = zrecv[0].astype(F32)
    for k in range(1, n_z):
        total = total + zrecv[k].astype(F32)
    zall[z] = total.astype(BF)
    z_start(lambda peer: zall.at[z], lambda i: zall.at[i], zb_ss, zb_rs)

    for piece, out in ((0, gout), (1, gin)):
        for source in range(n_z):
            merged = ((z == last) & (source == 0)) | ((z == 0) & (source == last))

            @pl.when((z != source) & jnp.logical_not(merged))
            def _():
                here = arrived.at[source, piece]
                remote(here, here, r_ss.at[0, piece], r_rs.at[source, piece], me, z).wait_recv()

        def finish(c, carry):
            at = rows_of(c, 128)
            total = dws[z, piece, at].astype(F32)
            for source in range(n_z):
                merged = ((z == last) & (source == 0)) | ((z == 0) & (source == last))
                counted = (z != source) & jnp.logical_not(merged)
                total = total + jnp.where(counted, arrived[source, piece, at].astype(F32), 0.0)
            out[at] = total
            return carry

        lax.fori_loop(0, 4, finish, 0)
    z_arrive(lambda i: zvec.at[i], zv_rs)
    gsmall[...] = zvec[0] + zvec[1] + zvec[2] + zvec[3]
    z_arrive(lambda i: zall.at[i], zb_rs)
    for k in range(n_z):
        piece = zall[k].astype(F32)
        gqkv[k * 16 : k * 16 + 16] = piece[:, 0:1536]
        gwo[k * 16 : k * 16 + 16] = piece[:, 1536:2048]
    own_gtok.wait()
    z_arrive(lambda i: gtok.at[pl.ds(i * im, im)], gt_rs)
    z_arrive(lambda i: mixed.at[pl.ds(i * im, im)], mix_rs)

    z_sent(lambda peer: xin.at[peer], tok_ss)
    z_sent(lambda peer: rin.at[peer], rts_ss)
    z_sent(lambda peer: tin.at[peer], tgt_ss)
    z_sent(lambda peer: mbuf.at[peer], gt_ss)
    z_sent(lambda peer: zsend.at[peer], za_ss)
    z_sent(lambda peer: zvec.at[peer], zv_ss)
    z_sent(lambda peer: zall.at[peer], zb_ss)
    dp_sent(dn_ss)
    weights_sent()
    for array in range(3):
        slot = dense_slot(array, 0)
        for k in range(half):
            remote(slot, slot, den_ss.at[array, k], loc_sem.at[8], me, z).wait_send()
        for k in range(1, half):
            remote(slot, slot, fwd_ss.at[array, k], loc_sem.at[8], me, z).wait_send()
    for piece in range(2):
        for target in range(n_z):
            here = dws.at[0, 0]

            @pl.when(z != target)
            def _():
                remote(here, here, r_ss.at[target, piece], loc_sem.at[8], me, z).wait_send()

    for q in range(half):
        remote(crecv.at[q], crecv.at[q], c_ss.at[q], loc_sem.at[8], me, z).wait_send()
    remote(cvec, cvec, cv_ss.at[0], loc_sem.at[8], me, z).wait_send()
    for k in range(1, half):
        remote(gsum.at[0], gsum.at[0], h_ss.at[k], loc_sem.at[8], me, z).wait_send()
        remote(cvec, cvec, hv_ss.at[k], loc_sem.at[8], me, z).wait_send()


def finish_kernel(mixed, gtok, gqkv, gwo, gsmall, gin, gout, *outs):
    me = lax.axis_index("dp")
    outs[0][...] = mixed[...]
    outs[1][...] = gtok[...].astype(F32)
    for source, target in ((gqkv, outs[2]), (gwo, outs[3]), (gin, outs[4]), (gout, outs[5])):
        target[...] = source[...]
    lanes = gsmall[:, pl.ds(pl.multiple_of((me // 2) * 128, 128), 128)]
    lanes = jnp.where(lax.rem(me, 2) == 1, pltpu.roll(lanes, 64, 1), lanes)
    outs[6][...] = lanes[:, 0:64]


def whole_images(
    tokens, ln1_gain, ln1_bias, w_qkv, w_out, ln2_gain, ln2_bias, w_router, expert_in, expert_out, routes, targets
):
    n_dp, n_z = lax.axis_size("dp"), lax.axis_size("seq")
    image_count, block, width = tokens.shape
    im = image_count // n_z
    cap = 2 * S // (n_z * w_router.shape[1]) + 2
    er = -(-(im * n_z * cap) // 16) * 16
    dims = (n_dp, n_z, im, block, cap, er)
    sp, nr, half = n_z * BP, n_dp * er, n_dp // 2
    me, z = lax.axis_index("dp"), lax.axis_index("seq")
    dma, vm = pltpu.SemaphoreType.DMA, pltpu.VMEM

    valid = z * block + jnp.arange(block) < VALID
    lines = jnp.where(valid[None, None, :], jnp.transpose(routes, (0, 2, 1)) + 1, 0)
    lines = jnp.pad(lines, ((0, 0), (0, 6), (0, BP - block)))
    odd = lax.rem(z, 2) == 1
    lines = jnp.concatenate([jnp.where(odd, 0, lines), jnp.where(odd, lines, 0)], axis=-1)
    vec = jnp.concatenate(
        [
            jnp.stack([ln1_gain, ln1_bias, ln2_gain, ln2_bias]),
            jnp.zeros((4, ln1_gain.shape[0]), BF),
            jnp.transpose(w_router),
        ],
        axis=0,
    )
    vec = lax.dynamic_update_slice(jnp.zeros((16, width), BF), vec, (0, me * ln1_gain.shape[0]))
    blocks = (n_z, im, block, width)
    in_any, in_vmem = pl.BlockSpec(memory_space=pl.ANY), pl.BlockSpec(memory_space=pltpu.VMEM)
    mixed, gtok, gqkv, gwo, gsmall, gin, gout = pl.pallas_call(
        functools.partial(block_kernel, dims),
        out_shape=[
            jax.ShapeDtypeStruct((image_count, block, width), BF),
            jax.ShapeDtypeStruct((image_count, block, width), BF),
            jax.ShapeDtypeStruct((64, 1536), F32),
            jax.ShapeDtypeStruct((64, width), F32),
            jax.ShapeDtypeStruct((16, width), F32),
            jax.ShapeDtypeStruct((512, 512), F32),
            jax.ShapeDtypeStruct((512, 512), F32),
        ],
        in_specs=[in_any, in_any, in_vmem, in_any, in_any, in_vmem, in_any, in_any],
        out_specs=[in_any, in_any] + [in_vmem] * 5,
        scratch_shapes=[
            vm(blocks, BF), vm((n_z, im, 8, 128), jnp.int32), vm(blocks, BF), vm((n_dp, 16, width), BF),
            vm((width, 1536), BF), vm((width, width), BF), vm((16, width), F32), vm((im, sp, width), BF),
            vm((im, sp, width), F32), vm((im, sp, width), BF), vm((im, sp, 1536), BF), vm((im, sp, width), BF),
            vm((im, sp, 128), F32), vm((im, 8, sp), F32), vm((im, 8, sp), F32), vm((im, sp, 128), F32),
            vm((n_z, 512, 512), BF), vm((n_z, 512, 512), BF), vm((nr, width), BF), vm((nr, width), BF),
            vm((n_z, nr, 512), BF), vm((n_z, nr, 512), BF), vm((n_dp, er, width), BF),
            vm(blocks, BF), vm((nr, width), BF), vm((im, sp, width), F32), vm((im, sp, 128), F32),
            vm((2, im, sp, width), BF), vm((nr, width), BF), vm((n_z, 2, 512, 512), BF), vm((n_z, 2, 512, 512), BF),
            vm((width, 2048), F32), vm((16, width), F32), vm((width, 2048), BF), vm((half, 64, 2048), BF),
            vm((16, width), F32), vm((half, 64, 2048), BF), vm((half, 64, 2048), BF), vm((half, 16, width), F32),
            vm((n_z, 16, 2048), BF), vm((n_z, 16, 2048), BF), vm((n_z, 16, 2048), BF), vm((n_z, 16, width), F32),
            dma((9,)), dma((n_z,)), dma((n_z,)), dma((n_z,)), dma((n_z,)), dma((n_z,)), dma((n_z,)),
            dma((3, half)), dma((3, n_dp)), dma((3, half)), dma((4,)), dma((n_z,)), dma((4,)), dma((n_z,)),
            dma((n_dp,)), dma((n_dp,)), dma((n_dp,)), dma((n_dp,)), dma((n_dp,)), dma((n_dp,)), dma((n_dp,)), dma((n_dp,)),
            dma((n_z,)), dma((n_z,)), dma((n_z,)), dma((n_z,)),
            dma((n_z, 2)), dma((n_z, 2)), dma((half,)), dma((half,)), dma((1,)), dma((1,)),
            dma((half,)), dma((half,)), dma((half,)), dma((half,)), dma((n_z,)), dma((n_z,)), dma((n_z,)), dma((n_z,)),
            dma((n_z,)), dma((n_z,)),
        ],
        compiler_params=pltpu.CompilerParams(
            collective_id=1, has_side_effects=True, vmem_limit_bytes=VMEM_LIMIT
        ),
        name="block",
    )(tokens, targets, lines, w_qkv, w_out, vec, expert_in[0], expert_out[0])
    whole = pl.BlockSpec(memory_space=pltpu.VMEM)
    mixed, gtok, gqkv, gwo, gin, gout, part = pl.pallas_call(
        finish_kernel,
        out_shape=[
            jax.ShapeDtypeStruct((image_count, block, width), BF),
            jax.ShapeDtypeStruct((image_count, block, width), F32),
            jax.ShapeDtypeStruct((64, 1536), F32),
            jax.ShapeDtypeStruct((64, width), F32),
            jax.ShapeDtypeStruct((512, 512), F32),
            jax.ShapeDtypeStruct((512, 512), F32),
            jax.ShapeDtypeStruct((16, 64), F32),
        ],
        in_specs=[whole] * 7,
        out_specs=[whole] * 7,
        name="finish",
    )(mixed, gtok, gqkv, gwo, gsmall, gin, gout)
    return (
        mixed,
        gtok,
        part[0],
        part[1],
        gqkv,
        gwo,
        part[2],
        part[3],
        jnp.transpose(part[8:16]),
        gin[None],
        gout[None],
    )


def fits(tokens, w_qkv, w_router, expert_in):
    n_dp, n_z = lax.axis_size("dp"), lax.axis_size("seq")
    return (
        n_dp == 8
        and n_z == 4
        and tokens.shape[0] % n_z == 0
        and tokens.shape[1] <= BP
        and tokens.shape[2] == 512
        and w_qkv.shape == (64, 1536)
        and w_router.shape[1] == n_dp
        and expert_in.shape == (1, 512, 512)
    )


def local(*args):
    if fits(args[0], args[3], args[7], args[8]):
        return whole_images(*args)
    return by_heads(*args)


def solution(mesh):
    placed = (
        P("dp", "seq", None),
        P("dp"),
        P("dp"),
        P("dp", None),
        P("dp", None),
        P("dp"),
        P("dp"),
        P("dp", None),
        P("dp", None, "seq"),
        P("dp", "seq", None),
        P("dp", "seq", None),
        P("dp", "seq", None),
    )
    return jax.shard_map(
        local,
        mesh=mesh,
        in_specs=placed,
        out_specs=(
            P("dp", "seq", None),
            P("dp", "seq", None),
            P("dp"),
            P("dp"),
            P("dp", None),
            P("dp", None),
            P("dp"),
            P("dp"),
            P("dp", None),
            P("dp", None, "seq"),
            P("dp", "seq", None),
        ),
        check_vma=False,
    )
```

profile of v0, /device:TPU:0, one launch (start us, length us, event | category | flops | bytes accessed | tf_op | source)
XLA Modules:
  0.0 244.4 jit_solution(4140241114206991653)
XLA Ops:
  0.7 1.4 concatenate.7
  2.1 0.7 select_bitcast_fusion
  2.8 0.2 dynamic_update_slice.3.vec
  3.0 0.0 copy-start
  3.0 0.7 pad_add_fusion.rts
  3.7 0.0 copy-done
  3.7 233.6 %block.1 = (bf16[12,50,512]{2,1,0:T(8,128)(2,1)}, bf16[12,50,512]{2,1,0:T(8,128)(2,1)}, f32[64,1536]{1,0:T(8,128)}, f32[64,512]{1,0:T(8,128)}, f32[16,512]{1,0:T...) custom-call(bf16[12,50,512]{2,1,0:T(8,128)(2,1)} %tok.1, bf16[12,50,512]{2,1,0:T(8,128)(2,1)} %tgt.1, ...), custom_call_target="tpu_custom_call" | custom-call | tf_op jit(solution)/shard_map/block/pallas_call | solution.py:1075
  237.4 4.4 %finish.1 = (bf16[12,50,512]{2,1,0:T(8,128)(2,1)}, f32[12,50,512]{2,1,0:T(8,128)}, f32[64,1536]{1,0:T(8,128)}, f32[64,512]{1,0:T(8,128)}, f32[512,512]{1,0:T(8,1...) custom-call(bf16[12,50,512]{2,1,0:T(8,128)(2,1)} %get-tuple-element.25.mixed, bf16[12,50,512]{2,1,0:T(8,128)(2,1)} %get-tuple-element.26.gtok, ...), custom_call_target="tpu_custom_call" | custom-call | tf_op jit(solution)/shard_map/finish/pallas_call | solution.py:1114
  241.8 1.4 slice_bitcast_fusion.1
  243.1 1.3 slice_bitcast_fusion
  (4 shorter events, 0.0 us)
Async XLA Ops:
  3.0 0.7 copy-start
where the time goes:
time: 245 us; the launch traced here: 244 us
  Pallas kernels  238 us (97%)
  local copies, waits for them, and re-layouts  4.23 us (2%)
    pallas_call x1, Pallas kernels, whole_images(): pl.pallas_call(functools.partial(block_kernel, dims), out_shape=[jax.Shap...  234 us

commit v1 on v0

--- a/solution.py
+++ b/solution.py
@@ -507,42 +507,44 @@
 
     experts = ((win, win_all, win_ss, win_rs), (wout, wout_all, wout_ss, wout_rs))
     inner = (z == 1) | (z == last - 1)
-    far_end = jnp.where(z == 1, last, 0)
-
-    def weight_send(array, kind, there, peer):
+    far_end = jnp.where(z < n_z // 2, last, 0)
+    near_end = last - far_end
+    middle = last - z
+
+    def gather_hop(array, step):
         source, full, send_sem, recv_sem = experts[array]
-
-        @pl.when(there)
-        def _():
-            remote(source, full.at[z], send_sem.at[kind], recv_sem.at[z], me, peer).start()
-
-    for array in range(2):
-        weight_send(array, 0, z >= 0, jnp.where(z < 2, z + 2, z - 2))
-    for array in range(2):
-        weight_send(array, 1, z < last, z + 1)
-        weight_send(array, 2, z > 0, z - 1)
-
-    def weight_wait(array, slot):
-        source, full, send_sem, recv_sem = experts[array]
-        at = full.at[slot]
-        remote(at, at, send_sem.at[0], recv_sem.at[slot], me, z).wait_recv()
-
-    def weight_forward(array):
-        source, full, send_sem, recv_sem = experts[array]
-
-        @pl.when(inner)
-        def _():
-            weight_wait(array, far_end)
-            at = full.at[far_end]
-            remote(at, at, send_sem.at[3], recv_sem.at[far_end], me, last - far_end).start()
-
-    def weights_sent():
-        for kind, there in ((0, z >= 0), (1, z < last), (2, z > 0), (3, inner)):
+        for way, there, slot in ((0, z >= step, z - step), (1, z + step < n_z, z + step)):
 
             @pl.when(there)
             def _():
-                for source, full, send_sem, recv_sem in experts:
-                    remote(full.at[0], full.at[0], send_sem.at[kind], recv_sem.at[0], me, z).wait_send()
+                at = full.at[slot]
+                if step > 0:
+                    remote(at, at, send_sem.at[way, step], recv_sem.at[slot], me, z).wait_recv()
+
+                @pl.when((z < last) if way == 0 else (z > 0))
+                def _():
+                    remote(
+                        at if step > 0 else source,
+                        at,
+                        send_sem.at[way, step],
+                        recv_sem.at[slot],
+                        me,
+                        z + 1 if way == 0 else z - 1,
+                    ).start()
+
+    def weights_sent():
+        for step in range(n_z - 1):
+            for way, there in ((0, (z >= step) & (z < last)), (1, (z + step < n_z) & (z > 0))):
+
+                @pl.when(there)
+                def _():
+                    for source, full, send_sem, recv_sem in experts:
+                        remote(
+                            full.at[0], full.at[0], send_sem.at[way, step], recv_sem.at[0], me, z
+                        ).wait_send()
+
+    gather_hop(0, 0)
+    gather_hop(1, 0)
 
     for k in range(1, half):
         origin = lax.rem(chip + k, half) * 2 + core
@@ -620,6 +622,11 @@
         table = jnp.concatenate(lines + [jnp.zeros((124, sp), F32)], axis=0)
         meta[i] = table[0:8]
         metat[i] = jnp.transpose(table)
+
+        @pl.when(i == im - 2)
+        def _():
+            gather_hop(0, 1)
+
         return carry
 
     lax.fori_loop(0, im, front, 0)
@@ -715,37 +722,30 @@
         lax.fori_loop(0, n_dp // 2, part_step, 0)
 
     def hidden_step(s, carry):
-        second = jnp.where(z == 0, 2, jnp.where(z == last, 1, last - far_end))
-        shard = jnp.where(
-            s == 0,
-            z,
-            jnp.where(
-                s == 1,
-                jnp.where(inner, far_end, jnp.where(z == 0, 1, last - 1)),
-                jnp.where(s == 2, second, last - z),
-            ),
-        )
-
-        @pl.when(inner & (s == 1))
+        for at_step, hop in ((1, 2), (3, 3)):
+
+            @pl.when(s == at_step)
+            def _():
+                gather_hop(0, hop)
+
+        for way in range(2):
+            shard = z - s if way == 0 else z + s
+
+            @pl.when((shard >= 0) & (shard < n_z) & ((s > 0) | (way == 0)))
+            def _():
+                hidden(shard)
+
+        @pl.when(s == 1)
         def _():
-            weight_forward(1)
-
-        @pl.when((s > 1) | ((s == 1) & jnp.logical_not(inner)))
-        def _():
-            weight_wait(0, shard)
-
-        hidden(shard)
+            gather_hop(1, 2)
+
         return carry
 
-    weight_forward(0)
+    gather_hop(1, 1)
     dp_arrive(recv, row_rs)
     dp_sent(row_ss)
     lax.fori_loop(0, n_z, hidden_step, 0)
-    for slot in range(n_z):
-
-        @pl.when((z != slot) & jnp.logical_not(inner & (far_end == slot)))
-        def _():
-            weight_wait(1, slot)
+    gather_hop(1, 3)
 
     z_start(tgt_of, lambda i: tin.at[i], tgt_ss, tgt_rs)
 
@@ -815,34 +815,38 @@
     dp_sent(du_ss)
 
     def reduce_start(target, piece):
-        held = inner & (target == far_end)
-        via = ((z == 0) & (target == last)) | ((z == last) & (target == 0))
-        peer = jnp.where(via, jnp.where(z == 0, 1, last - 1), target)
-
-        @pl.when((target != z) & jnp.logical_not(held))
-        def _():
-            slot = jnp.where(via, peer, z)
-            remote(
-                dws.at[target, piece], arrived.at[slot, piece], r_ss.at[target, piece], r_rs.at[slot, piece], me, peer
-            ).start()
-
-    def reduce_forward(piece):
+        peer = jnp.where(z == 0, 1, last - 1)
+        slot = jnp.where(target == peer, 0, jnp.where(target == far_end, 2, 1))
+        remote(
+            dws.at[target, piece], arrived.at[slot, piece], r_ss.at[target, piece], r_rs.at[slot, piece], me, peer
+        ).start()
+
+    def reduce_forward(piece, steps):
         @pl.when(inner)
         def _():
-            here = arrived.at[z, piece]
-            remote(here, here, r_ss.at[far_end, piece], r_rs.at[z, piece], me, z).wait_recv()
-
-            def add(c, carry):
-                at = rows_of(c, 128)
-                dws[far_end, piece, at] = (
-                    dws[far_end, piece, at].astype(F32) + arrived[z, piece, at].astype(F32)
-                ).astype(BF)
-                return carry
-
-            lax.fori_loop(0, 4, add, 0)
-            remote(
-                dws.at[far_end, piece], here, r_ss.at[far_end, piece], r_rs.at[z, piece], me, far_end
-            ).start()
+            for target, slot, peer, there in steps:
+                here = arrived.at[slot, piece]
+                remote(here, here, r_ss.at[target, piece], r_rs.at[slot, piece], me, z).wait_recv()
+
+                def add(c, carry):
+                    at = rows_of(c, 128)
+                    dws[target, piece, at] = (
+                        dws[target, piece, at].astype(F32) + arrived[slot, piece, at].astype(F32)
+                    ).astype(BF)
+                    return carry
+
+                lax.fori_loop(0, 4, add, 0)
+                remote(
+                    dws.at[target, piece],
+                    arrived.at[there, piece],
+                    r_ss.at[target, piece],
+                    r_rs.at[there, piece],
+                    me,
+                    peer,
+                ).start()
+
+    first_steps = ((far_end, 2, middle, 4),)
+    second_steps = ((middle, 1, middle, 3), (near_end, 4, near_end, 0))
 
     def owner(s):
         return jnp.where(z < n_z // 2, lax.rem(z + 2 * n_z - 1 - s, n_z), lax.rem(z + 1 + s, n_z))
@@ -850,13 +854,21 @@
     def out_grads(s, carry):
         target = owner(s)
         dws[target, 0] = tn(acts[target], drows[...]).astype(BF)
-        reduce_start(target, 0)
+
+        @pl.when(jnp.logical_not(inner) & (s < 2))
+        def _():
+            reduce_start(target, 0)
+
         return carry
 
     def in_grads(s, carry):
         target = owner(s)
         dws[target, 1] = tn(recv[...], slopes[target]).astype(BF)
-        reduce_start(target, 1)
+
+        @pl.when(jnp.logical_not(inner) & (s < 2))
+        def _():
+            reduce_start(target, 1)
+
         return carry
 
     lax.fori_loop(0, n_z, out_grads, 0)
@@ -873,10 +885,17 @@
 
     to_tokens(input_grads_for, dret, dn_ss, dn_rs)
     lax.fori_loop(0, n_z, in_grads, 0)
+
+    @pl.when(jnp.logical_not(inner))
+    def _():
+        reduce_start(owner(2), 0)
+        reduce_start(owner(2), 1)
+
+    reduce_forward(0, first_steps)
     own_mixed.wait()
     z_sent(lambda peer: mbuf.at[peer], mix_ss)
     dp_arrive(dret, dn_rs)
-    reduce_forward(0)
+    reduce_forward(0, second_steps)
 
     def back(i, carry):
         line = lax.broadcasted_iota(jnp.int32, (sp, nr), 1).astype(F32)
@@ -924,12 +943,14 @@
         dx = (dx2 + norm_back(dn1 * gain_one, hat1, scale1)).astype(BF)
         for b in range(n_z):
             mbuf[b, i] = dx[b * BP : b * BP + block]
+
+        @pl.when(i == im - 2)
+        def _():
+            reduce_forward(1, first_steps)
+
         return carry
 
     lax.fori_loop(0, im, back, 0)
-    z_start(lambda peer: mbuf.at[peer], lambda i: gtok.at[pl.ds(i * im, im)], gt_ss, gt_rs)
-    own_gtok = pltpu.make_async_copy(mbuf.at[z], gtok.at[pl.ds(z * im, im)], loc_sem.at[1])
-    own_gtok.start()
 
     gbig[...] = gacc[...].astype(BF)
     for q in range(half):
@@ -948,55 +969,90 @@
     for k in range(1, half):
         q = lax.rem(chip + k, half)
         remote(hvec.at[chip], hvec.at[chip], hv_ss.at[k], hv_rs.at[chip], q * 2 + core, z).start()
-    reduce_forward(1)
+    reduce_forward(1, second_steps)
     dense = gacc[rows_of(me, 64)] + crecv[chip].astype(F32)
     for k in range(1, half):
         q = lax.rem(chip + k, half)
         remote(hrecv.at[q], hrecv.at[q], h_ss.at[0], h_rs.at[q], me, z).wait_recv()
         dense = dense + hrecv[q].astype(F32)
-    for peer in range(n_z):
-        zsend[peer] = dense[peer * 16 : peer * 16 + 16].astype(BF)
-    z_start(lambda peer: zsend.at[peer], lambda i: zrecv.at[i], za_ss, za_rs)
+    for h in range(2):
+        zsend[h] = dense[h * 32 : h * 32 + 32].astype(BF)
+
+        @pl.when(z == h + 1)
+        def _():
+            zrecv[z] = zsend[h]
+
+        @pl.when(z != h + 1)
+        def _():
+            remote(zsend.at[h], zrecv.at[z], za_ss.at[h], za_rs.at[z], me, h + 1).start()
+
     for k in range(1, half):
         q = lax.rem(chip + k, half)
         remote(hvec.at[q], hvec.at[q], hv_ss.at[0], hv_rs.at[q], me, z).wait_recv()
     zvec[z] = hvec[0] + hvec[1] + hvec[2] + hvec[3]
-    z_start(lambda peer: zvec.at[z], lambda i: zvec.at[i], zv_ss, zv_rs)
-    zrecv[z] = zsend[z]
-    z_arrive(lambda i: zrecv.at[i], za_rs)
-    total = zrecv[0].astype(F32)
-    for k in range(1, n_z):
-        total = total + zrecv[k].astype(F32)
-    zall[z] = total.astype(BF)
-    z_start(lambda peer: zall.at[z], lambda i: zall.at[i], zb_ss, zb_rs)
+
+    @pl.when(z != 1)
+    def _():
+        remote(zvec.at[z], zvec.at[z], zv_ss.at[0], zv_rs.at[z], me, 1).start()
+
+    z_start(lambda peer: mbuf.at[peer], lambda i: gtok.at[pl.ds(i * im, im)], gt_ss, gt_rs)
+    own_gtok = pltpu.make_async_copy(mbuf.at[z], gtok.at[pl.ds(z * im, im)], loc_sem.at[1])
+    own_gtok.start()
 
     for piece, out in ((0, gout), (1, gin)):
-        for source in range(n_z):
-            merged = ((z == last) & (source == 0)) | ((z == 0) & (source == last))
-
-            @pl.when((z != source) & jnp.logical_not(merged))
+        for slot, there in ((0, z >= 0), (3, inner)):
+
+            @pl.when(there)
             def _():
-                here = arrived.at[source, piece]
-                remote(here, here, r_ss.at[0, piece], r_rs.at[source, piece], me, z).wait_recv()
+                here = arrived.at[slot, piece]
+                remote(here, here, r_ss.at[0, piece], r_rs.at[slot, piece], me, z).wait_recv()
 
         def finish(c, carry):
             at = rows_of(c, 128)
-            total = dws[z, piece, at].astype(F32)
-            for source in range(n_z):
-                merged = ((z == last) & (source == 0)) | ((z == 0) & (source == last))
-                counted = (z != source) & jnp.logical_not(merged)
-                total = total + jnp.where(counted, arrived[source, piece, at].astype(F32), 0.0)
-            out[at] = total
+            out[at] = (
+                dws[z, piece, at].astype(F32)
+                + arrived[0, piece, at].astype(F32)
+                + jnp.where(inner, arrived[3, piece, at].astype(F32), 0.0)
+            )
             return carry
 
         lax.fori_loop(0, 4, finish, 0)
-    z_arrive(lambda i: zvec.at[i], zv_rs)
-    gsmall[...] = zvec[0] + zvec[1] + zvec[2] + zvec[3]
-    z_arrive(lambda i: zall.at[i], zb_rs)
-    for k in range(n_z):
-        piece = zall[k].astype(F32)
-        gqkv[k * 16 : k * 16 + 16] = piece[:, 0:1536]
-        gwo[k * 16 : k * 16 + 16] = piece[:, 1536:2048]
+    for h in range(2):
+
+        @pl.when(z == h + 1)
+        def _():
+            z_arrive(lambda i: zrecv.at[i], za_rs)
+            total = zrecv[0].astype(F32)
+            for k in range(1, n_z):
+                total = total + zrecv[k].astype(F32)
+            zall[h] = total.astype(BF)
+            for k in range(1, n_z):
+                peer = lax.rem(z + k, n_z)
+                remote(zall.at[h], zall.at[h], zb_ss.at[k], zb_rs.at[h], me, peer).start()
+
+    @pl.when(z == 1)
+    def _():
+        z_arrive(lambda i: zvec.at[i], zv_rs)
+        gsmall[...] = zvec[0] + zvec[1] + zvec[2] + zvec[3]
+        zvec[n_z] = gsmall[...]
+        for k in range(1, n_z):
+            peer = lax.rem(z + k, n_z)
+            remote(zvec.at[n_z], zvec.at[n_z], zv_ss.at[k], zv_rs.at[n_z], me, peer).start()
+
+    @pl.when(z != 1)
+    def _():
+        remote(zvec.at[n_z], zvec.at[n_z], zv_ss.at[0], zv_rs.at[n_z], me, z).wait_recv()
+        gsmall[...] = zvec[n_z]
+
+    for h in range(2):
+
+        @pl.when(z != h + 1)
+        def _():
+            remote(zall.at[h], zall.at[h], zb_ss.at[0], zb_rs.at[h], me, z).wait_recv()
+
+        piece = zall[h].astype(F32)
+        gqkv[h * 32 : h * 32 + 32] = piece[:, 0:1536]
+        gwo[h * 32 : h * 32 + 32] = piece[:, 1536:2048]
     own_gtok.wait()
     z_arrive(lambda i: gtok.at[pl.ds(i * im, im)], gt_rs)
     z_arrive(lambda i: mixed.at[pl.ds(i * im, im)], mix_rs)
@@ -1005,9 +1061,24 @@
     z_sent(lambda peer: rin.at[peer], rts_ss)
     z_sent(lambda peer: tin.at[peer], tgt_ss)
     z_sent(lambda peer: mbuf.at[peer], gt_ss)
-    z_sent(lambda peer: zsend.at[peer], za_ss)
-    z_sent(lambda peer: zvec.at[peer], zv_ss)
-    z_sent(lambda peer: zall.at[peer], zb_ss)
+    for h in range(2):
+
+        @pl.when(z != h + 1)
+        def _():
+            remote(zsend.at[h], zsend.at[h], za_ss.at[h], loc_sem.at[8], me, z).wait_send()
+
+        @pl.when(z == h + 1)
+        def _():
+            z_sent(lambda peer: zall.at[0], zb_ss)
+
+    @pl.when(z == 1)
+    def _():
+        z_sent(lambda peer: zvec.at[0], zv_ss)
+
+    @pl.when(z != 1)
+    def _():
+        remote(zvec.at[0], zvec.at[0], zv_ss.at[0], loc_sem.at[8], me, z).wait_send()
+
     dp_sent(dn_ss)
     weights_sent()
     for array in range(3):
@@ -1093,17 +1164,17 @@
             vm((n_z, 512, 512), BF), vm((n_z, 512, 512), BF), vm((nr, width), BF), vm((nr, width), BF),
             vm((n_z, nr, 512), BF), vm((n_z, nr, 512), BF), vm((n_dp, er, width), BF),
             vm(blocks, BF), vm((nr, width), BF), vm((im, sp, width), F32), vm((im, sp, 128), F32),
-            vm((2, im, sp, width), BF), vm((nr, width), BF), vm((n_z, 2, 512, 512), BF), vm((n_z, 2, 512, 512), BF),
+            vm((2, im, sp, width), BF), vm((nr, width), BF), vm((n_z, 2, 512, 512), BF), vm((5, 2, 512, 512), BF),
             vm((width, 2048), F32), vm((16, width), F32), vm((width, 2048), BF), vm((half, 64, 2048), BF),
             vm((16, width), F32), vm((half, 64, 2048), BF), vm((half, 64, 2048), BF), vm((half, 16, width), F32),
-            vm((n_z, 16, 2048), BF), vm((n_z, 16, 2048), BF), vm((n_z, 16, 2048), BF), vm((n_z, 16, width), F32),
+            vm((2, 32, 2048), BF), vm((n_z, 32, 2048), BF), vm((2, 32, 2048), BF), vm((n_z + 1, 16, width), F32),
             dma((9,)), dma((n_z,)), dma((n_z,)), dma((n_z,)), dma((n_z,)), dma((n_z,)), dma((n_z,)),
-            dma((3, half)), dma((3, n_dp)), dma((3, half)), dma((4,)), dma((n_z,)), dma((4,)), dma((n_z,)),
+            dma((3, half)), dma((3, n_dp)), dma((3, half)), dma((2, n_z)), dma((n_z,)), dma((2, n_z)), dma((n_z,)),
             dma((n_dp,)), dma((n_dp,)), dma((n_dp,)), dma((n_dp,)), dma((n_dp,)), dma((n_dp,)), dma((n_dp,)), dma((n_dp,)),
             dma((n_z,)), dma((n_z,)), dma((n_z,)), dma((n_z,)),
-            dma((n_z, 2)), dma((n_z, 2)), dma((half,)), dma((half,)), dma((1,)), dma((1,)),
-            dma((half,)), dma((half,)), dma((half,)), dma((half,)), dma((n_z,)), dma((n_z,)), dma((n_z,)), dma((n_z,)),
-            dma((n_z,)), dma((n_z,)),
+            dma((n_z, 2)), dma((5, 2)), dma((half,)), dma((half,)), dma((1,)), dma((1,)),
+            dma((half,)), dma((half,)), dma((half,)), dma((half,)), dma((2,)), dma((n_z,)), dma((n_z,)), dma((2,)),
+            dma((n_z,)), dma((n_z + 1,)),
         ],
         compiler_params=pltpu.CompilerParams(
             collective_id=1, has_side_effects=True, vmem_limit_bytes=VMEM_LIMIT

time: 245 us -> 235 us (0.959)
  Pallas kernels: 238 us -> 227 us
    pallas_call x1, Pallas kernels: 234 us -> 223 us  [whole_images(): pl.pallas_call(functools.partial(block_kernel, dims), out_shape=[jax.Shap...]
where the time goes in v1:
time: 235 us; the launch traced here: 234 us
  Pallas kernels  227 us (97%)
  local copies, waits for them, and re-layouts  4.23 us (2%)
    pallas_call x1, Pallas kernels, whole_images(): pl.pallas_call(functools.partial(block_kernel, dims), out_shape=[jax.Shap...  223 us

profile of v1, /device:TPU:0, one launch (start us, length us, event | category | flops | bytes accessed | tf_op | source)
XLA Modules:
  0.0 233.6 jit_solution(1859824936888516819)
XLA Ops:
  0.7 1.4 concatenate.7
  2.1 0.7 select_bitcast_fusion
  2.8 0.2 dynamic_update_slice.3.vec
  3.0 0.0 copy-start
  3.0 0.7 pad_add_fusion.rts
  3.7 0.0 copy-done
  3.7 222.8 %block.1 = (bf16[12,50,512]{2,1,0:T(8,128)(2,1)}, bf16[12,50,512]{2,1,0:T(8,128)(2,1)}, f32[64,1536]{1,0:T(8,128)}, f32[64,512]{1,0:T(8,128)}, f32[16,512]{1,0:T...) custom-call(bf16[12,50,512]{2,1,0:T(8,128)(2,1)} %tok.1, bf16[12,50,512]{2,1,0:T(8,128)(2,1)} %tgt.1, ...), custom_call_target="tpu_custom_call" | custom-call | tf_op jit(solution)/shard_map/block/pallas_call | solution.py:1146
  226.5 4.4 %finish.1 = (bf16[12,50,512]{2,1,0:T(8,128)(2,1)}, f32[12,50,512]{2,1,0:T(8,128)}, f32[64,1536]{1,0:T(8,128)}, f32[64,512]{1,0:T(8,128)}, f32[512,512]{1,0:T(8,1...) custom-call(bf16[12,50,512]{2,1,0:T(8,128)(2,1)} %get-tuple-element.25.mixed, bf16[12,50,512]{2,1,0:T(8,128)(2,1)} %get-tuple-element.26.gtok, ...), custom_call_target="tpu_custom_call" | custom-call | tf_op jit(solution)/shard_map/finish/pallas_call | solution.py:1185
  230.9 1.4 slice_bitcast_fusion.1
  232.3 1.3 slice_bitcast_fusion
  (4 shorter events, 0.0 us)
Async XLA Ops:
  3.0 0.7 copy-start

commit v2 on v1

--- a/solution.py
+++ b/solution.py
@@ -427,33 +427,143 @@
     dims,
     tok, tgt, rts, wq, wo, vec, win, wout,
     mixed, gtok, gqkv, gwo, gsmall, gin, gout,
-    xin, rin, tin, vec_all, wq_all, wo_all, vsum, xpad, x2s, n2s, qkvs, outs, lses, gts, meta, metat,
+    xin, rin, tin, vec_all, wq_all, wo_all, vsum, xpad, n2s, qkvs, outs, cols, gts, meta,
     win_all, wout_all, recv, ret, acts, slopes, sbuf,
-    mbuf, drows, dys, dlogs, dus, dret, dws, arrived,
-    gacc, gvec, gbig, crecv, cvec, gsum, hrecv, hvec, zsend, zrecv, zall, zvec,
+    drows, dys, dws, arrived,
+    gacc, gvec, csend, crecv, cvec, hrecv, hvec, zsend, zrecv, zall, zvec,
     loc_sem, tok_ss, tok_rs, rts_ss, rts_rs, tgt_ss, tgt_rs, den_ss, den_rs, fwd_ss, win_ss, win_rs, wout_ss, wout_rs,
     row_ss, row_rs, u_ss, u_rs, du_ss, du_rs, dn_ss, dn_rs, mix_ss, mix_rs, gt_ss, gt_rs,
     r_ss, r_rs, c_ss, c_rs, cv_ss, cv_rs, h_ss, h_rs, hv_ss, hv_rs, za_ss, za_rs, zb_ss, zb_rs, zv_ss, zv_rs,
 ):
-    n_dp, n_z, im, block, cap, er = dims
+    n_dp, n_z, counts, block, cap = dims
+    firsts = tuple(sum(counts[:h]) for h in range(n_z))
     me, z = lax.axis_index("dp"), lax.axis_index("seq")
     sp = n_z * BP
-    nr = n_dp * er
-    two = 2 * er
     half = n_dp // 2
     last = n_z - 1
     core, chip = lax.rem(me, 2), me // 2
     partner = chip * 2 + 1 - core
+    inner = (z == 1) | (z == last - 1)
+    ends = jnp.logical_not(inner)
+    far_end = jnp.where(z < n_z // 2, last, 0)
+    near_end = last - far_end
+    middle = last - z
+    im = jnp.where(inner, counts[1], counts[0])
+    sizes = ((counts[1], inner), (counts[0], ends))
+    first = jnp.where(z == 0, firsts[0], jnp.where(z == 1, firsts[1], jnp.where(z == 2, firsts[2], firsts[3])))
 
     barrier = pltpu.get_barrier_semaphore()
     for k in range(1, n_dp):
         pl.semaphore_signal(barrier, inc=1, device_id=(lax.rem(me + k, n_dp), z), device_id_type=MESH_ID)
     for k in range(1, n_z):
         pl.semaphore_signal(barrier, inc=1, device_id=(me, lax.rem(z + k, n_z)), device_id_type=MESH_ID)
+
+    def hosts_own(source, target, sem):
+        for h in range(n_z):
+
+            @pl.when(z == h)
+            def _():
+                pltpu.make_async_copy(
+                    source.at[pl.ds(firsts[h], counts[h])], target.at[z, pl.ds(0, counts[h])], sem
+                ).start()
+
+    def hosts_own_wait(source, target, sem):
+        for h in range(n_z):
+
+            @pl.when(z == h)
+            def _():
+                pltpu.make_async_copy(
+                    source.at[pl.ds(firsts[h], counts[h])], target.at[z, pl.ds(0, counts[h])], sem
+                ).wait()
+
+    def hosts_start(source, target, send_sem, recv_sem, hosts, who):
+        for h in hosts:
+
+            @pl.when((z != h) & who)
+            def _():
+                remote(
+                    source.at[pl.ds(firsts[h], counts[h])],
+                    target.at[z, pl.ds(0, counts[h])],
+                    send_sem.at[h],
+                    recv_sem.at[z],
+                    me,
+                    h,
+                ).start()
+
+    def hosts_arrive(target, recv_sem):
+        for size, there in sizes:
+
+            @pl.when(there)
+            def _():
+                for k in range(1, n_z):
+                    origin = lax.rem(z + k, n_z)
+                    spot = target.at[origin, pl.ds(0, size)]
+                    remote(spot, spot, loc_sem.at[8], recv_sem.at[origin], me, z).wait_recv()
+
+    def hosts_sent(target, send_sem):
+        for h in range(n_z):
+
+            @pl.when(z != h)
+            def _():
+                spot = target.at[0, pl.ds(0, counts[h])]
+                remote(spot, spot, send_sem.at[h], loc_sem.at[8], me, z).wait_send()
+
+    def home_own(source, target, sem):
+        return [
+            (there, pltpu.make_async_copy(source.at[z, pl.ds(0, size)], target.at[pl.ds(first, size)], sem))
+            for size, there in sizes
+        ]
+
+    def home_start(source, target, send_sem, recv_sem, who):
+        for size, there in who:
+
+            @pl.when(there)
+            def _():
+                for k in range(1, n_z):
+                    peer = lax.rem(z + k, n_z)
+                    remote(
+                        source.at[peer, pl.ds(0, size)],
+                        target.at[pl.ds(first, size)],
+                        send_sem.at[k],
+                        recv_sem.at[z],
+                        me,
+                        peer,
+                    ).start()
+
+    def home_arrive(target, recv_sem):
+        for h in range(n_z):
+
+            @pl.when(z != h)
+            def _():
+                spot = target.at[pl.ds(firsts[h], counts[h])]
+                remote(spot, spot, loc_sem.at[8], recv_sem.at[h], me, z).wait_recv()
+
+    def home_sent(source, send_sem):
+        for size, there in sizes:
+
+            @pl.when(there)
+            def _():
+                for k in range(1, n_z):
+                    spot = source.at[0, pl.ds(0, size)]
+                    remote(spot, spot, send_sem.at[k], loc_sem.at[8], me, z).wait_send()
+
+    def each(pairs, act):
+        for there, copy in pairs:
+
+            @pl.when(there)
+            def _():
+                getattr(copy, act)()
+
+    def z_arrive(target, recv_sem):
+        for k in range(1, n_z):
+            origin = lax.rem(z + k, n_z)
+            remote(target(origin), target(origin), loc_sem.at[8], recv_sem.at[origin], me, z).wait_recv()
+
+    def z_sent(source, send_sem):
+        for k in range(1, n_z):
+            remote(source(0), source(0), send_sem.at[k], loc_sem.at[8], me, z).wait_send()
+
     own_copies = [
-        pltpu.make_async_copy(tok.at[pl.ds(z * im, im)], xin.at[z], loc_sem.at[0]),
-        pltpu.make_async_copy(rts.at[pl.ds(z * im, im)], rin.at[z], loc_sem.at[1]),
-        pltpu.make_async_copy(tgt.at[pl.ds(z * im, im)], tin.at[z], loc_sem.at[2]),
         pltpu.make_async_copy(win, win_all.at[z], loc_sem.at[3]),
         pltpu.make_async_copy(wout, wout_all.at[z], loc_sem.at[4]),
         pltpu.make_async_copy(wq, wq_all.at[rows_of(me, 64)], loc_sem.at[5]),
@@ -462,30 +572,14 @@
     ]
     for copy in own_copies:
         copy.start()
-    xpad[...] = jnp.zeros_like(xpad)
-    gacc[...] = jnp.zeros_like(gacc)
-    gvec[...] = jnp.zeros_like(gvec)
+    hosts_own(tok, xin, loc_sem.at[0])
+    hosts_own(rts, rin, loc_sem.at[1])
+    hosts_own(tgt, tin, loc_sem.at[2])
+    for buffer in (xpad, gacc, gvec, recv, ret, drows):
+        buffer[...] = jnp.zeros_like(buffer)
     pl.semaphore_wait(barrier, n_dp + n_z - 2)
-
-    def z_start(source, target, send_sem, recv_sem):
-        for k in range(1, n_z):
-            peer = lax.rem(z + k, n_z)
-            remote(source(peer), target(z), send_sem.at[k], recv_sem.at[z], me, peer).start()
-
-    def z_arrive(target, recv_sem):
-        for k in range(1, n_z):
-            origin = lax.rem(z + k, n_z)
-            remote(target(origin), target(origin), loc_sem.at[8], recv_sem.at[origin], me, z).wait_recv()
-
-    def z_sent(source, send_sem):
-        for k in range(1, n_z):
-            remote(source(0), source(0), send_sem.at[k], loc_sem.at[8], me, z).wait_send()
-
-    tok_of = lambda peer: tok.at[pl.ds(peer * im, im)]
-    rts_of = lambda peer: rts.at[pl.ds(peer * im, im)]
-    tgt_of = lambda peer: tgt.at[pl.ds(peer * im, im)]
-    z_start(tok_of, lambda i: xin.at[i], tok_ss, tok_rs)
-    z_start(rts_of, lambda i: rin.at[i], rts_ss, rts_rs)
+    hosts_start(tok, xin, tok_ss, tok_rs, range(n_z), z >= 0)
+    hosts_start(rts, rin, rts_ss, rts_rs, range(n_z), z >= 0)
 
     def dense_slot(array, index):
         if array == 0:
@@ -506,10 +600,6 @@
         ).start()
 
     experts = ((win, win_all, win_ss, win_rs), (wout, wout_all, wout_ss, wout_rs))
-    inner = (z == 1) | (z == last - 1)
-    far_end = jnp.where(z < n_z // 2, last, 0)
-    near_end = last - far_end
-    middle = last - z
 
     def gather_hop(array, step):
         source, full, send_sem, recv_sem = experts[array]
@@ -559,12 +649,15 @@
             remote(slot, slot, den_ss.at[array, 0], den_rs.at[array, origin], me, z).wait_recv()
     for copy in own_copies:
         copy.wait()
+    hosts_own_wait(tok, xin, loc_sem.at[0])
+    hosts_own_wait(rts, rin, loc_sem.at[1])
+    hosts_own_wait(tgt, tin, loc_sem.at[2])
     total = vec_all[0].astype(F32)
     for k in range(1, n_dp):
         total = total + vec_all[k].astype(F32)
     vsum[...] = total
-    z_arrive(lambda i: xin.at[i], tok_rs)
-    z_arrive(lambda i: rin.at[i], rts_rs)
+    hosts_arrive(xin, tok_rs)
+    hosts_arrive(rin, rts_rs)
 
     masks = half_masks()
     keys_ok = slot_ok(lax.broadcasted_iota(jnp.int32, (1, sp), 1), block)
@@ -574,6 +667,49 @@
     router_t = vsum[8:16, :].astype(BF)
     lane_id = lax.broadcasted_iota(jnp.int32, (sp, 128), 1)
     lane_low = lane_id < 64
+    row_id = lax.broadcasted_iota(jnp.int32, (512, sp), 0).astype(F32)
+
+    def rows_at(index):
+        return pl.ds(pl.multiple_of(index * 64, 64), n_z * cap)
+
+    def send_rows(i, target, send_sem, recv_sem):
+        def step(s, carry):
+            j, c = lax.rem(s // 2 + 1, half), lax.rem(s, 2)
+            index = 2 * j + c
+            peer = lax.rem(chip + j, half) * 2 + lax.rem(core + c, 2)
+
+            @pl.when(index > 0)
+            def _():
+                remote(
+                    sbuf.at[i, rows_at(peer)],
+                    target.at[i, rows_at(me)],
+                    send_sem.at[i, index],
+                    recv_sem.at[i, me],
+                    peer,
+                    z,
+                ).start()
+
+            return carry
+
+        lax.fori_loop(0, n_dp, step, 0)
+        target[i, rows_of(me, 64)] = sbuf[i, rows_of(me, 64)]
+
+    def arrive(i, target, recv_sem):
+        def step(k, carry):
+            origin = lax.rem(me + k, n_dp)
+            spot = target.at[i, rows_at(origin)]
+            remote(spot, spot, loc_sem.at[8], recv_sem.at[i, origin], me, z).wait_recv()
+            return carry
+
+        lax.fori_loop(1, n_dp, step, 0)
+
+    def sent(i, send_sem):
+        def step(index, carry):
+            spot = sbuf.at[i, rows_at(0)]
+            remote(spot, spot, send_sem.at[i, index], loc_sem.at[8], me, z).wait_send()
+            return carry
+
+        lax.fori_loop(1, n_dp, step, 0)
 
     def front(i, carry):
         before = lax.broadcasted_iota(jnp.int32, (sp, sp), 0)
@@ -602,9 +738,7 @@
                 lse_all = jnp.where(lane_id == pair * 2 + side, top + jnp.log(whole), lse_all)
                 parts.append(nn((exponent / whole).astype(BF), v2))
             outs[i, :, pair * 128 : pair * 128 + 128] = jnp.where(lane_low, parts[0], parts[1]).astype(BF)
-        lses[i] = lse_all
         x2 = x + nn(outs[i], wo_all[...])
-        x2s[i] = x2
         hat2, _ = norm_parts(x2)
         n2 = (hat2 * gain_two + bias_two).astype(BF)
         n2s[i] = n2
@@ -616,14 +750,18 @@
         hits = [(expert_id + 1) == wide[j : j + 1, :] for j in range(2)]
         any_hit = jnp.where(hits[0] | hits[1], 1.0, 0.0)
         place = nn(any_hit.astype(BF), prefix)
-        base = place + (expert_id * er + (slot_lane // BP) * cap + i * (n_z * cap) + 1).astype(F32)
+        base = place + (expert_id * 64 + (slot_lane // BP) * cap + 1).astype(F32)
         lines = [jnp.sum(jnp.where(hit, base, 0.0), axis=0, keepdims=True) - 1.0 for hit in hits]
         lines += [jnp.sum(jnp.where(hit, share, 0.0), axis=0, keepdims=True) for hit in hits]
-        table = jnp.concatenate(lines + [jnp.zeros((124, sp), F32)], axis=0)
-        meta[i] = table[0:8]
-        metat[i] = jnp.transpose(table)
-
-        @pl.when(i == im - 2)
+        lines = jnp.concatenate(lines + [jnp.zeros((4, sp), F32)], axis=0)
+        meta[i] = lines
+        table = jnp.concatenate([jnp.zeros((8, sp), F32), lines, jnp.zeros((112, sp), F32)], axis=0)
+        cols[i] = jnp.transpose(table) + lse_all
+        pick = (row_id == lines[0:1, :]) | (row_id == lines[1:2, :])
+        sbuf[i] = nn(jnp.where(pick, 1.0, 0.0).astype(BF), n2).astype(BF)
+        send_rows(i, recv, row_ss, row_rs)
+
+        @pl.when(i == 1)
         def _():
             gather_hop(0, 1)
 
@@ -631,95 +769,22 @@
 
     lax.fori_loop(0, im, front, 0)
 
-    row_id = lax.broadcasted_iota(jnp.int32, (er, sp), 0)
-
-    def to_experts(product, target, send_sem, recv_sem):
-        def step(s, carry):
-            j, c = lax.rem(s // 2 + 1, half), lax.rem(s, 2)
-            index = 2 * j + c
-            peer = lax.rem(chip + j, half) * 2 + lax.rem(core + c, 2)
-            sbuf[index] = product(peer).astype(BF)
-
-            @pl.when(index > 0)
-            def _():
-                remote(
-                    sbuf.at[index], target.at[rows_of(me, er)], send_sem.at[index], recv_sem.at[me], peer, z
-                ).start()
-
-            @pl.when(index == 0)
-            def _():
-                target[rows_of(me, er)] = sbuf[index]
-
-            return carry
-
-        lax.fori_loop(0, n_dp, step, 0)
-
-    def to_tokens(product, target, send_sem, recv_sem):
-        def step(s, carry):
-            j = lax.rem(s + 1, half)
-            part = lax.rem(chip + j, half)
-            out = product(part).astype(BF)
-            sbuf[2 * j] = out[0:er]
-            sbuf[2 * j + 1] = out[er:two]
-
-            @pl.when(j > 0)
-            def _():
-                for c in range(2):
-                    remote(
-                        sbuf.at[2 * j + c],
-                        target.at[rows_of(me, er)],
-                        send_sem.at[2 * j + c],
-                        recv_sem.at[me],
-                        part * 2 + c,
-                        z,
-                    ).start()
-
-            @pl.when(j == 0)
-            def _():
-                target[rows_of(me, er)] = sbuf[core]
-                remote(
-                    sbuf.at[1 - core], target.at[rows_of(me, er)], send_sem.at[1], recv_sem.at[me], partner, z
-                ).start()
-
-            return carry
-
-        lax.fori_loop(0, half, step, 0)
-
-    def dp_arrive(target, recv_sem):
-        for k in range(1, n_dp):
-            origin = lax.rem(me + k, n_dp)
-            spot = target.at[rows_of(origin, er)]
-            remote(spot, spot, loc_sem.at[8], recv_sem.at[origin], me, z).wait_recv()
-
-    def dp_sent(send_sem):
-        for k in range(1, n_dp):
-            remote(sbuf.at[0], sbuf.at[0], send_sem.at[k], loc_sem.at[8], me, z).wait_send()
-
-    def tokens_for(peer):
-        want = (row_id + peer * er).astype(F32)
-        total = jnp.zeros((er, 512), F32)
-        for i in range(im):
-            pick = (want == meta[i, 0:1, :]) | (want == meta[i, 1:2, :])
-            total = total + nn(jnp.where(pick, 1.0, 0.0).astype(BF), n2s[i])
-        return total
-
-    to_experts(tokens_for, recv, row_ss, row_rs)
+    hosts_start(tgt, tin, tgt_ss, tgt_rs, (1, 2), z >= 0)
 
     def hidden(shard):
-        def part_step(part, carry):
-            at = rows_of(part, two)
-            x = recv[at]
+        def image(i, carry):
+            x = recv[i]
             for side in range(2):
                 pre = nn(x, win_all[shard, :, side * 256 : side * 256 + 256])
                 square = pre * pre
                 tanh = jnp.tanh(pre * (GELU_C + (GELU_C * GELU_K) * square))
                 gate = 0.5 + 0.5 * tanh
-                acts[shard, at, side * 256 : side * 256 + 256] = (pre * gate).astype(BF)
+                acts[shard, i, :, side * 256 : side * 256 + 256] = (pre * gate).astype(BF)
                 slope = gate + pre * (0.5 - 0.5 * tanh * tanh) * (GELU_C + (3.0 * GELU_C * GELU_K) * square)
-                slopes[shard, at, side * 256 : side * 256 + 256] = slope.astype(BF)
+                slopes[shard, i, :, side * 256 : side * 256 + 256] = slope.astype(BF)
             return carry
 
-        lax.fori_loop(0, n_dp // 2, part_step, 0)
+        lax.fori_loop(0, im, image, 0)
 
     def hidden_step(s, carry):
         for at_step, hop in ((1, 2), (3, 3)):
@@ -735,84 +800,92 @@
             def _():
                 hidden(shard)
 
-        @pl.when(s == 1)
+        @pl.when(s == 2)
         def _():
             gather_hop(1, 2)
 
         return carry
 
     gather_hop(1, 1)
-    dp_arrive(recv, row_rs)
-    dp_sent(row_ss)
+
+    def rows_here(i, carry):
+        arrive(i, recv, row_rs)
+        return carry
+
+    lax.fori_loop(0, im, rows_here, 0)
     lax.fori_loop(0, n_z, hidden_step, 0)
     gather_hop(1, 3)
 
-    z_start(tgt_of, lambda i: tin.at[i], tgt_ss, tgt_rs)
-
-    def results_for(part):
-        total = jnp.zeros((two, 512), F32)
-        for shard in range(n_z):
-            total = total + nn(acts[shard, rows_of(part, two)], wout_all[shard])
-        return total
-
-    to_tokens(results_for, ret, u_ss, u_rs)
-
-    z_arrive(lambda i: tin.at[i], tgt_rs)
-    for b in range(n_z):
-        for i in range(im):
-            dys[i, b * BP : b * BP + block, :] = tin[b, i].astype(F32)
-    dp_arrive(ret, u_rs)
+    hosts_start(tgt, tin, tgt_ss, tgt_rs, (0, last), ends)
+
+    def results(i, carry):
+        total = nn(acts[0, i], wout_all[0])
+        for shard in range(1, n_z):
+            total = total + nn(acts[shard, i], wout_all[shard])
+        sent(i, row_ss)
+        sbuf[i] = total.astype(BF)
+        send_rows(i, ret, u_ss, u_rs)
+        return carry
+
+    lax.fori_loop(0, im, results, 0)
 
     def mix(i, carry):
-        line = lax.broadcasted_iota(jnp.int32, (sp, nr), 1).astype(F32)
-        cols = metat[i]
+        @pl.when(i == 1)
+        def _():
+            hosts_start(tgt, tin, tgt_ss, tgt_rs, (0, last), inner)
+
+        arrive(i, ret, u_rs)
+
+        @pl.when(i == 0)
+        def _():
+            hosts_arrive(tin, tgt_rs)
+
+        line = lax.broadcasted_iota(jnp.int32, (sp, 512), 1).astype(F32)
+        here = cols[i]
         picked = []
         for j in range(2):
-            pick = jnp.where(line == cols[:, j : j + 1], 1.0, 0.0).astype(BF)
-            picked.append(nn(pick, ret[...]))
-        mix = x2s[i] + cols[:, 2:3] * picked[0] + cols[:, 3:4] * picked[1]
+            pick = jnp.where(line == here[:, 8 + j : 9 + j], 1.0, 0.0).astype(BF)
+            picked.append(nn(pick, ret[i]))
+        x2 = xpad[i].astype(F32) + nn(outs[i], wo_all[...])
+        mix = x2 + here[:, 10:11] * picked[0] + here[:, 11:12] * picked[1]
         mix_b = mix.astype(BF)
         for b in range(n_z):
-            mbuf[b, i] = mix_b[b * BP : b * BP + block]
+            xin[b, i] = mix_b[b * BP : b * BP + block]
+            dys[i, b * BP : b * BP + block, :] = tin[b, i].astype(F32)
         dy = jnp.where(rows_ok, mix - dys[i], 0.0)
         dys[i] = dy
-        dus[0, i] = (cols[:, 2:3] * dy).astype(BF)
-        dus[1, i] = (cols[:, 3:4] * dy).astype(BF)
-        dlogs[i] = jnp.where(
-            lane_id == 0, jnp.sum(dy * picked[0], axis=-1, keepdims=True), 0.0
-        ) + jnp.where(lane_id == 1, jnp.sum(dy * picked[1], axis=-1, keepdims=True), 0.0)
+        total = jnp.zeros((512, 512), F32)
+        for j in range(2):
+            pick = jnp.where(row_id == meta[i, j : j + 1, :], 1.0, 0.0).astype(BF)
+            total = total + nn(pick, (here[:, 10 + j : 11 + j] * dy).astype(BF))
+        sent(i, u_ss)
+        sbuf[i] = total.astype(BF)
+        send_rows(i, drows, du_ss, du_rs)
+        for j in range(2):
+            here = jnp.where(lane_id == 12 + j, jnp.sum(dy * picked[j], axis=-1, keepdims=True), here)
+        cols[i] = here
         return carry
 
     lax.fori_loop(0, im, mix, 0)
-    dp_sent(u_ss)
-
-    def gradients_for(peer):
-        want = (row_id + peer * er).astype(F32)
-        total = jnp.zeros((er, 512), F32)
-        for i in range(im):
-            for j in range(2):
-                pick = jnp.where(want == meta[i, j : j + 1, :], 1.0, 0.0).astype(BF)
-                total = total + nn(pick, dus[j, i])
-        return total
-
-    to_experts(gradients_for, drows, du_ss, du_rs)
-    z_start(lambda peer: mbuf.at[peer], lambda i: mixed.at[pl.ds(i * im, im)], mix_ss, mix_rs)
-    own_mixed = pltpu.make_async_copy(mbuf.at[z], mixed.at[pl.ds(z * im, im)], loc_sem.at[0])
-    own_mixed.start()
+    home_start(xin, mixed, mix_ss, mix_rs, sizes)
+    own_mixed = home_own(xin, mixed, loc_sem.at[0])
+    each(own_mixed, "start")
     expert_row = lax.broadcasted_iota(jnp.int32, (8, sp), 0).astype(F32)
-    for i in range(im):
-        flat = jnp.transpose(dlogs[i])
+
+    def gates_back(i, carry):
+        flat = jnp.transpose(cols[i])
         share = gts[i]
         grad = jnp.zeros((8, sp), F32)
         for j in range(2):
             at = meta[i, j : j + 1, :]
-            inside = (at >= expert_row * er) & (at < expert_row * er + er)
-            grad = grad + jnp.where(inside, flat[j : j + 1, :], 0.0)
+            inside = (at >= expert_row * 64) & (at < expert_row * 64 + 64)
+            grad = grad + jnp.where(inside, flat[12 + j : 13 + j, :], 0.0)
         dlog = share * (grad - jnp.sum(share * grad, axis=0, keepdims=True))
         gts[i] = dlog
         gvec[8:16, :] += nn(dlog.astype(BF), n2s[i])
-    dp_arrive(drows, du_rs)
-    dp_sent(du_ss)
+        return carry
+
+    lax.fori_loop(0, im, gates_back, 0)
 
     def reduce_start(target, piece):
         peer = jnp.where(z == 0, 1, last - 1)
@@ -851,58 +924,73 @@
     def owner(s):
         return jnp.where(z < n_z // 2, lax.rem(z + 2 * n_z - 1 - s, n_z), lax.rem(z + 1 + s, n_z))
 
-    def out_grads(s, carry):
+    def lanes_of(target):
+        return pl.ds(pl.multiple_of(target * 512, 512), 512)
+
+    def out_ready(s, carry):
         target = owner(s)
-        dws[target, 0] = tn(acts[target], drows[...]).astype(BF)
-
-        @pl.when(jnp.logical_not(inner) & (s < 2))
+        dws[target, 0] = gacc[:, lanes_of(target)].astype(BF)
+
+        @pl.when(ends & (s < 2))
         def _():
             reduce_start(target, 0)
 
         return carry
+
+    def experts_back(i, carry):
+        arrive(i, drows, du_rs)
+        du = drows[i]
+        for target in range(n_z):
+            gacc[:, target * 512 : target * 512 + 512] += tn(acts[target, i], du)
+
+        @pl.when(i == im - 1)
+        def _():
+            lax.fori_loop(0, n_z, out_ready, 0)
+
+        total = jnp.zeros((512, 512), F32)
+        for shard in range(n_z):
+            dpre = (nt(du, wout_all[shard]) * slopes[shard, i].astype(F32)).astype(BF)
+            slopes[shard, i] = dpre
+            total = total + nt(dpre, win_all[shard])
+        sent(i, du_ss)
+        sbuf[i] = total.astype(BF)
+        send_rows(i, ret, dn_ss, dn_rs)
+        return carry
+
+    lax.fori_loop(0, im, experts_back, 0)
+    reduce_forward(0, first_steps)
 
     def in_grads(s, carry):
         target = owner(s)
-        dws[target, 1] = tn(recv[...], slopes[target]).astype(BF)
-
-        @pl.when(jnp.logical_not(inner) & (s < 2))
+        gacc[:, 0:512] = tn(recv[0], slopes[target, 0])
+
+        def more(i, carry):
+            gacc[:, 0:512] += tn(recv[i], slopes[target, i])
+            return carry
+
+        lax.fori_loop(1, im, more, 0)
+        dws[target, 1] = gacc[:, 0:512].astype(BF)
+
+        @pl.when(ends & (s < 2))
         def _():
             reduce_start(target, 1)
 
         return carry
 
-    lax.fori_loop(0, n_z, out_grads, 0)
-
-    def input_grads_for(part):
-        at = rows_of(part, two)
-        du = drows[at]
-        total = jnp.zeros((two, 512), F32)
-        for shard in range(n_z):
-            dpre = (nt(du, wout_all[shard]) * slopes[shard, at].astype(F32)).astype(BF)
-            slopes[shard, at] = dpre
-            total = total + nt(dpre, win_all[shard])
-        return total
-
-    to_tokens(input_grads_for, dret, dn_ss, dn_rs)
     lax.fori_loop(0, n_z, in_grads, 0)
 
-    @pl.when(jnp.logical_not(inner))
-    def _():
-        reduce_start(owner(2), 0)
-        reduce_start(owner(2), 1)
-
-    reduce_forward(0, first_steps)
-    own_mixed.wait()
-    z_sent(lambda peer: mbuf.at[peer], mix_ss)
-    dp_arrive(dret, dn_rs)
+    gacc[...] = jnp.zeros_like(gacc)
+    each(own_mixed, "wait")
+    home_sent(xin, mix_ss)
     reduce_forward(0, second_steps)
 
     def back(i, carry):
-        line = lax.broadcasted_iota(jnp.int32, (sp, nr), 1).astype(F32)
-        cols = metat[i]
-        pick = jnp.where((line == cols[:, 0:1]) | (line == cols[:, 1:2]), 1.0, 0.0).astype(BF)
-        dn2 = nn(pick, dret[...]) + tn(gts[i].astype(BF), router_t)
-        hat2, scale2 = norm_parts(x2s[i])
+        arrive(i, ret, dn_rs)
+        line = lax.broadcasted_iota(jnp.int32, (sp, 512), 1).astype(F32)
+        here = cols[i]
+        pick = jnp.where((line == here[:, 8:9]) | (line == here[:, 9:10]), 1.0, 0.0).astype(BF)
+        dn2 = nn(pick, ret[i]) + tn(gts[i].astype(BF), router_t)
+        hat2, scale2 = norm_parts(xpad[i].astype(F32) + nn(outs[i], wo_all[...]))
         gvec[2:3, :] += jnp.sum(dn2 * hat2, axis=0, keepdims=True)
         gvec[3:4, :] += jnp.sum(dn2, axis=0, keepdims=True)
         dx2 = dys[i] + norm_back(dn2 * gain_two, hat2, scale2)
@@ -911,7 +999,6 @@
         do = nt(da, wo_all[...]).astype(BF)
         hat1, scale1 = norm_parts(xpad[i].astype(F32))
         n1 = (hat1 * gain_one + bias_one).astype(BF)
-        dn1 = jnp.zeros((sp, 512), F32)
         for pair in range(4):
             at = pair * 128
             q2 = qkvs[i, :, at : at + 128]
@@ -923,7 +1010,7 @@
                 head = pair * 2 + side
                 scores = nt(q2 * masks[side], k2) * 0.125
                 scores = jnp.where(keys_ok, scores, NEG)
-                prob = jnp.exp(scores - lses[i, :, head : head + 1])
+                prob = jnp.exp(scores - here[:, head : head + 1])
                 dprob = nt(do2 * masks[side], v2)
                 inner = jnp.sum(prob * dprob, axis=-1, keepdims=True)
                 ds = (prob * (dprob - inner)).astype(BF)
@@ -934,42 +1021,46 @@
                 grad = jnp.where(lane_low, grads[part][0], grads[part][1])
                 if part < 2:
                     grad = grad * 0.125
-                grad = grad.astype(BF)
-                col = part * 512 + at
-                gacc[:, col : col + 128] += tn(n1, grad)
-                dn1 = dn1 + nt(grad, wq_all[:, col : col + 128])
+                qkvs[i, :, part * 512 + at : part * 512 + at + 128] = grad.astype(BF)
+        dqkv = qkvs[i]
+        gacc[:, 0:1536] += tn(n1, dqkv)
+        dn1 = nt(dqkv, wq_all[...])
         gvec[0:1, :] += jnp.sum(dn1 * hat1, axis=0, keepdims=True)
         gvec[1:2, :] += jnp.sum(dn1, axis=0, keepdims=True)
         dx = (dx2 + norm_back(dn1 * gain_one, hat1, scale1)).astype(BF)
         for b in range(n_z):
-            mbuf[b, i] = dx[b * BP : b * BP + block]
-
-        @pl.when(i == im - 2)
+            xin[b, i] = dx[b * BP : b * BP + block]
+
+        @pl.when(i == 0)
         def _():
             reduce_forward(1, first_steps)
 
+        @pl.when(i == 1)
+        def _():
+            reduce_forward(1, second_steps)
+
         return carry
 
     lax.fori_loop(0, im, back, 0)
-
-    gbig[...] = gacc[...].astype(BF)
+    home_start(xin, gtok, gt_ss, gt_rs, sizes[:1])
+    own_gtok = home_own(xin, gtok, loc_sem.at[1])
+    each(own_gtok, "start")
+
     for q in range(half):
-        remote(
-            gbig.at[rows_of(2 * q + 1 - core, 64)], crecv.at[q], c_ss.at[q], c_rs.at[q], partner, z
-        ).start()
+        csend[q] = gacc[rows_of(2 * q + 1 - core, 64)].astype(BF)
+        remote(csend.at[q], crecv.at[q], c_ss.at[q], c_rs.at[q], partner, z).start()
     remote(gvec, cvec, cv_ss.at[0], cv_rs.at[0], partner, z).start()
     for q in range(half):
         remote(crecv.at[q], crecv.at[q], c_ss.at[q], c_rs.at[q], me, z).wait_recv()
     for k in range(1, half):
         q = lax.rem(chip + k, half)
-        gsum[q] = (gacc[rows_of(2 * q + core, 64)] + crecv[q].astype(F32)).astype(BF)
-        remote(gsum.at[q], hrecv.at[chip], h_ss.at[k], h_rs.at[chip], q * 2 + core, z).start()
+        crecv[q] = (gacc[rows_of(2 * q + core, 64)] + crecv[q].astype(F32)).astype(BF)
+        remote(crecv.at[q], hrecv.at[chip], h_ss.at[k], h_rs.at[chip], q * 2 + core, z).start()
     remote(cvec, cvec, cv_ss.at[0], cv_rs.at[0], me, z).wait_recv()
     hvec[chip] = gvec[...] + cvec[...]
     for k in range(1, half):
         q = lax.rem(chip + k, half)
         remote(hvec.at[chip], hvec.at[chip], hv_ss.at[k], hv_rs.at[chip], q * 2 + core, z).start()
-    reduce_forward(1, second_steps)
     dense = gacc[rows_of(me, 64)] + crecv[chip].astype(F32)
     for k in range(1, half):
         q = lax.rem(chip + k, half)
@@ -995,11 +1086,18 @@
     def _():
         remote(zvec.at[z], zvec.at[z], zv_ss.at[0], zv_rs.at[z], me, 1).start()
 
-    z_start(lambda peer: mbuf.at[peer], lambda i: gtok.at[pl.ds(i * im, im)], gt_ss, gt_rs)
-    own_gtok = pltpu.make_async_copy(mbuf.at[z], gtok.at[pl.ds(z * im, im)], loc_sem.at[1])
-    own_gtok.start()
-
-    for piece, out in ((0, gout), (1, gin)):
+    @pl.when(ends)
+    def _():
+        reduce_start(owner(2), 0)
+        reduce_start(owner(2), 1)
+
+    home_start(xin, gtok, gt_ss, gt_rs, sizes[1:])
+
+    final_copies = [
+        pltpu.make_async_copy(gacc.at[:, pl.ds(piece * 512, 512)], out, loc_sem.at[2 + piece])
+        for piece, out in ((0, gout), (1, gin))
+    ]
+    for piece in range(2):
         for slot, there in ((0, z >= 0), (3, inner)):
 
             @pl.when(there)
@@ -1009,7 +1107,7 @@
 
         def finish(c, carry):
             at = rows_of(c, 128)
-            out[at] = (
+            gacc[at, piece * 512 : piece * 512 + 512] = (
                 dws[z, piece, at].astype(F32)
                 + arrived[0, piece, at].astype(F32)
                 + jnp.where(inner, arrived[3, piece, at].astype(F32), 0.0)
@@ -1017,6 +1115,7 @@
             return carry
 
         lax.fori_loop(0, 4, finish, 0)
+        final_copies[piece].start()
     for h in range(2):
 
         @pl.when(z == h + 1)
@@ -1053,14 +1152,16 @@
         piece = zall[h].astype(F32)
         gqkv[h * 32 : h * 32 + 32] = piece[:, 0:1536]
         gwo[h * 32 : h * 32 + 32] = piece[:, 1536:2048]
-    own_gtok.wait()
-    z_arrive(lambda i: gtok.at[pl.ds(i * im, im)], gt_rs)
-    z_arrive(lambda i: mixed.at[pl.ds(i * im, im)], mix_rs)
-
-    z_sent(lambda peer: xin.at[peer], tok_ss)
-    z_sent(lambda peer: rin.at[peer], rts_ss)
-    z_sent(lambda peer: tin.at[peer], tgt_ss)
-    z_sent(lambda peer: mbuf.at[peer], gt_ss)
+    each(own_gtok, "wait")
+    home_arrive(gtok, gt_rs)
+    home_arrive(mixed, mix_rs)
+    for copy in final_copies:
+        copy.wait()
+
+    hosts_sent(xin, tok_ss)
+    hosts_sent(rin, rts_ss)
+    hosts_sent(tin, tgt_ss)
+    home_sent(xin, gt_ss)
     for h in range(2):
 
         @pl.when(z != h + 1)
@@ -1079,7 +1180,12 @@
     def _():
         remote(zvec.at[0], zvec.at[0], zv_ss.at[0], loc_sem.at[8], me, z).wait_send()
 
-    dp_sent(dn_ss)
+
+    def rows_sent(i, carry):
+        sent(i, dn_ss)
+        return carry
+
+    lax.fori_loop(0, im, rows_sent, 0)
     weights_sent()
     for array in range(3):
         slot = dense_slot(array, 0)
@@ -1099,7 +1205,7 @@
         remote(crecv.at[q], crecv.at[q], c_ss.at[q], loc_sem.at[8], me, z).wait_send()
     remote(cvec, cvec, cv_ss.at[0], loc_sem.at[8], me, z).wait_send()
     for k in range(1, half):
-        remote(gsum.at[0], gsum.at[0], h_ss.at[k], loc_sem.at[8], me, z).wait_send()
+        remote(crecv.at[0], crecv.at[0], h_ss.at[k], loc_sem.at[8], me, z).wait_send()
         remote(cvec, cvec, hv_ss.at[k], loc_sem.at[8], me, z).wait_send()
 
 
@@ -1119,11 +1225,10 @@
 ):
     n_dp, n_z = lax.axis_size("dp"), lax.axis_size("seq")
     image_count, block, width = tokens.shape
-    im = image_count // n_z
+    im = image_count // 3
     cap = 2 * S // (n_z * w_router.shape[1]) + 2
-    er = -(-(im * n_z * cap) // 16) * 16
-    dims = (n_dp, n_z, im, block, cap, er)
-    sp, nr, half = n_z * BP, n_dp * er, n_dp // 2
+    dims = (n_dp, n_z, (image_count // 6, im, im, image_count // 6), block, cap)
+    sp, half = n_z * BP, n_dp // 2
     me, z = lax.axis_index("dp"), lax.axis_index("seq")
     dma, vm = pltpu.SemaphoreType.DMA, pltpu.VMEM
 
@@ -1155,22 +1260,22 @@
             jax.ShapeDtypeStruct((512, 512), F32),
         ],
         in_specs=[in_any, in_any, in_vmem, in_any, in_any, in_vmem, in_any, in_any],
-        out_specs=[in_any, in_any] + [in_vmem] * 5,
+        out_specs=[in_any, in_any] + [in_vmem] * 3 + [in_any] * 2,
         scratch_shapes=[
             vm(blocks, BF), vm((n_z, im, 8, 128), jnp.int32), vm(blocks, BF), vm((n_dp, 16, width), BF),
             vm((width, 1536), BF), vm((width, width), BF), vm((16, width), F32), vm((im, sp, width), BF),
-            vm((im, sp, width), F32), vm((im, sp, width), BF), vm((im, sp, 1536), BF), vm((im, sp, width), BF),
-            vm((im, sp, 128), F32), vm((im, 8, sp), F32), vm((im, 8, sp), F32), vm((im, sp, 128), F32),
-            vm((n_z, 512, 512), BF), vm((n_z, 512, 512), BF), vm((nr, width), BF), vm((nr, width), BF),
-            vm((n_z, nr, 512), BF), vm((n_z, nr, 512), BF), vm((n_dp, er, width), BF),
-            vm(blocks, BF), vm((nr, width), BF), vm((im, sp, width), F32), vm((im, sp, 128), F32),
-            vm((2, im, sp, width), BF), vm((nr, width), BF), vm((n_z, 2, 512, 512), BF), vm((5, 2, 512, 512), BF),
-            vm((width, 2048), F32), vm((16, width), F32), vm((width, 2048), BF), vm((half, 64, 2048), BF),
-            vm((16, width), F32), vm((half, 64, 2048), BF), vm((half, 64, 2048), BF), vm((half, 16, width), F32),
+            vm((im, sp, width), BF), vm((im, sp, 1536), BF), vm((im, sp, width), BF),
+            vm((im, sp, 128), F32), vm((im, 8, sp), F32), vm((im, 8, sp), F32),
+            vm((n_z, 512, 512), BF), vm((n_z, 512, 512), BF), vm((im, 512, 512), BF), vm((im, 512, 512), BF),
+            vm((n_z, im, 512, 512), BF), vm((n_z, im, 512, 512), BF), vm((im, 512, 512), BF),
+            vm((im, 512, 512), BF), vm((im, sp, width), F32), vm((n_z, 2, 512, 512), BF), vm((5, 2, 512, 512), BF),
+            vm((width, 2048), F32), vm((16, width), F32), vm((half, 64, 2048), BF), vm((half, 64, 2048), BF),
+            vm((16, width), F32), vm((half, 64, 2048), BF), vm((half, 16, width), F32),
             vm((2, 32, 2048), BF), vm((n_z, 32, 2048), BF), vm((2, 32, 2048), BF), vm((n_z + 1, 16, width), F32),
             dma((9,)), dma((n_z,)), dma((n_z,)), dma((n_z,)), dma((n_z,)), dma((n_z,)), dma((n_z,)),
             dma((3, half)), dma((3, n_dp)), dma((3, half)), dma((2, n_z)), dma((n_z,)), dma((2, n_z)), dma((n_z,)),
-            dma((n_dp,)), dma((n_dp,)), dma((n_dp,)), dma((n_dp,)), dma((n_dp,)), dma((n_dp,)), dma((n_dp,)), dma((n_dp,)),
+            dma((im, n_dp)), dma((im, n_dp)), dma((im, n_dp)), dma((im, n_dp)), dma((im, n_dp)), dma((im, n_dp)),
+            dma((im, n_dp)), dma((im, n_dp)),
             dma((n_z,)), dma((n_z,)), dma((n_z,)), dma((n_z,)),
             dma((n_z, 2)), dma((5, 2)), dma((half,)), dma((half,)), dma((1,)), dma((1,)),
             dma((half,)), dma((half,)), dma((half,)), dma((half,)), dma((2,)), dma((n_z,)), dma((n_z,)), dma((2,)),
@@ -1217,7 +1322,7 @@
     return (
         n_dp == 8
         and n_z == 4
-        and tokens.shape[0] % n_z == 0
+        and tokens.shape[0] % 6 == 0
         and tokens.shape[1] <= BP
         and tokens.shape[2] == 512
         and w_qkv.shape == (64, 1536)

time: 235 us -> 225 us (0.957)
  Pallas kernels: 227 us -> 218 us
    pallas_call x1, Pallas kernels: 223 us -> 213 us  [whole_images(): pl.pallas_call(functools.partial(block_kernel, dims), out_shape=[jax.Shap...]
where the time goes in v2:
time: 225 us; the launch traced here: 224 us
  Pallas kernels  218 us (97%)
  local copies, waits for them, and re-layouts  4.23 us (2%)
    pallas_call x1, Pallas kernels, whole_images(): pl.pallas_call(functools.partial(block_kernel, dims), out_shape=[jax.Shap...  213 us

profile of v2, /device:TPU:0, one launch (start us, length us, event | category | flops | bytes accessed | tf_op | source)
XLA Modules:
  0.0 224.0 jit_solution(8600857460905052678)
XLA Ops:
  0.7 1.4 concatenate.7
  2.1 0.7 select_bitcast_fusion
  2.8 0.2 dynamic_update_slice.3.vec
  3.0 0.0 copy-start
  3.0 0.7 pad_add_fusion.rts
  3.7 0.0 copy-done
  3.7 213.2 %block.1 = (bf16[12,50,512]{2,1,0:T(8,128)(2,1)}, bf16[12,50,512]{2,1,0:T(8,128)(2,1)}, f32[64,1536]{1,0:T(8,128)}, f32[64,512]{1,0:T(8,128)}, f32[16,512]{1,0:T...) custom-call(bf16[12,50,512]{2,1,0:T(8,128)(2,1)} %tok.1, bf16[12,50,512]{2,1,0:T(8,128)(2,1)} %tgt.1, ...), custom_call_target="tpu_custom_call" | custom-call | tf_op jit(solution)/shard_map/block/pallas_call | solution.py:1251
  216.9 4.4 %finish.1 = (bf16[12,50,512]{2,1,0:T(8,128)(2,1)}, f32[12,50,512]{2,1,0:T(8,128)}, f32[64,1536]{1,0:T(8,128)}, f32[64,512]{1,0:T(8,128)}, f32[512,512]{1,0:T(8,1...) custom-call(bf16[12,50,512]{2,1,0:T(8,128)(2,1)} %get-tuple-element.25.mixed, bf16[12,50,512]{2,1,0:T(8,128)(2,1)} %get-tuple-element.26.gtok, ...), custom_call_target="tpu_custom_call" | custom-call | tf_op jit(solution)/shard_map/finish/pallas_call | solution.py:1290
  221.3 1.4 slice_bitcast_fusion.1
  222.7 1.3 slice_bitcast_fusion
  (4 shorter events, 0.0 us)
Async XLA Ops:
  3.0 0.7 copy-start

commit v3 on v2

--- a/solution.py
+++ b/solution.py
@@ -414,9 +414,8 @@
 
 def half_masks():
     lane = lax.broadcasted_iota(jnp.int32, (1, 128), 1)
-    low = jnp.where(lane < 64, 1.0, 0.0).astype(BF)
-    high = jnp.where(lane < 64, 0.0, 1.0).astype(BF)
-    return (low, high)
+    low = jnp.where(lane < 64, 1.0, 0.0)
+    return (low.astype(BF), (1.0 - low).astype(BF))
 
 
 def slot_ok(position, block):
@@ -430,7 +429,7 @@
     xin, rin, tin, vec_all, wq_all, wo_all, vsum, xpad, n2s, qkvs, outs, cols, gts, meta,
     win_all, wout_all, recv, ret, acts, slopes, sbuf,
     drows, dys, dws, arrived,
-    gacc, gvec, csend, crecv, cvec, hrecv, hvec, zsend, zrecv, zall, zvec,
+    gacc, accf, gvec, csend, crecv, cvec, hrecv, hvec, zsend, zrecv, zall, zvec,
     loc_sem, tok_ss, tok_rs, rts_ss, rts_rs, tgt_ss, tgt_rs, den_ss, den_rs, fwd_ss, win_ss, win_rs, wout_ss, wout_rs,
     row_ss, row_rs, u_ss, u_rs, du_ss, du_rs, dn_ss, dn_rs, mix_ss, mix_rs, gt_ss, gt_rs,
     r_ss, r_rs, c_ss, c_rs, cv_ss, cv_rs, h_ss, h_rs, hv_ss, hv_rs, za_ss, za_rs, zb_ss, zb_rs, zv_ss, zv_rs,
@@ -554,15 +553,6 @@
             def _():
                 getattr(copy, act)()
 
-    def z_arrive(target, recv_sem):
-        for k in range(1, n_z):
-            origin = lax.rem(z + k, n_z)
-            remote(target(origin), target(origin), loc_sem.at[8], recv_sem.at[origin], me, z).wait_recv()
-
-    def z_sent(source, send_sem):
-        for k in range(1, n_z):
-            remote(source(0), source(0), send_sem.at[k], loc_sem.at[8], me, z).wait_send()
-
     own_copies = [
         pltpu.make_async_copy(win, win_all.at[z], loc_sem.at[3]),
         pltpu.make_async_copy(wout, wout_all.at[z], loc_sem.at[4]),
@@ -575,7 +565,7 @@
     hosts_own(tok, xin, loc_sem.at[0])
     hosts_own(rts, rin, loc_sem.at[1])
     hosts_own(tgt, tin, loc_sem.at[2])
-    for buffer in (xpad, gacc, gvec, recv, ret, drows):
+    for buffer in (xpad, gvec, recv, ret, drows):
         buffer[...] = jnp.zeros_like(buffer)
     pl.semaphore_wait(barrier, n_dp + n_z - 2)
     hosts_start(tok, xin, tok_ss, tok_rs, range(n_z), z >= 0)
@@ -660,6 +650,7 @@
     hosts_arrive(rin, rts_rs)
 
     masks = half_masks()
+    eighths = [mask * 0.125 for mask in masks]
     keys_ok = slot_ok(lax.broadcasted_iota(jnp.int32, (1, sp), 1), block)
     rows_ok = slot_ok(lax.broadcasted_iota(jnp.int32, (sp, 1), 0), block)
     gain_one, bias_one = vsum[0:1, :], vsum[1:2, :]
@@ -668,6 +659,9 @@
     lane_id = lax.broadcasted_iota(jnp.int32, (sp, 128), 1)
     lane_low = lane_id < 64
     row_id = lax.broadcasted_iota(jnp.int32, (512, sp), 0).astype(F32)
+
+    def lanes_of(target):
+        return pl.ds(pl.multiple_of(target * 512, 512), 512)
 
     def rows_at(index):
         return pl.ds(pl.multiple_of(index * 64, 64), n_z * cap)
@@ -730,7 +724,7 @@
             v2 = qkvs[i, :, 1024 + pair * 128 : 1024 + pair * 128 + 128]
             parts = []
             for side in range(2):
-                scores = nt(q2 * masks[side], k2) * 0.125
+                scores = nt(q2 * eighths[side], k2)
                 scores = jnp.where(keys_ok, scores, NEG)
                 top = jnp.max(scores, axis=-1, keepdims=True)
                 exponent = jnp.exp(scores - top)
@@ -769,7 +763,6 @@
 
     lax.fori_loop(0, im, front, 0)
 
-    hosts_start(tgt, tin, tgt_ss, tgt_rs, (1, 2), z >= 0)
 
     def hidden(shard):
         def image(i, carry):
@@ -803,6 +796,7 @@
         @pl.when(s == 2)
         def _():
             gather_hop(1, 2)
+            hosts_start(tgt, tin, tgt_ss, tgt_rs, (1, 2), z >= 0)
 
         return carry
 
@@ -814,20 +808,29 @@
 
     lax.fori_loop(0, im, rows_here, 0)
     lax.fori_loop(0, n_z, hidden_step, 0)
+
+    def early_results(i, carry):
+        for k in range(1, n_z):
+            shard = lax.rem(far_end + k, n_z)
+            part = nn(acts[shard, i], wout_all[shard])
+            if k == 1:
+                gacc[:, lanes_of(i)] = part
+            else:
+                gacc[:, lanes_of(i)] += part
+        return carry
+
+    lax.fori_loop(0, im, early_results, 0)
     gather_hop(1, 3)
-
     hosts_start(tgt, tin, tgt_ss, tgt_rs, (0, last), ends)
 
     def results(i, carry):
-        total = nn(acts[0, i], wout_all[0])
-        for shard in range(1, n_z):
-            total = total + nn(acts[shard, i], wout_all[shard])
         sent(i, row_ss)
-        sbuf[i] = total.astype(BF)
+        sbuf[i] = (gacc[:, lanes_of(i)] + nn(acts[far_end, i], wout_all[far_end])).astype(BF)
         send_rows(i, ret, u_ss, u_rs)
         return carry
 
     lax.fori_loop(0, im, results, 0)
+    gacc[...] = jnp.zeros_like(gacc)
 
     def mix(i, carry):
         @pl.when(i == 1)
@@ -924,9 +927,6 @@
     def owner(s):
         return jnp.where(z < n_z // 2, lax.rem(z + 2 * n_z - 1 - s, n_z), lax.rem(z + 1 + s, n_z))
 
-    def lanes_of(target):
-        return pl.ds(pl.multiple_of(target * 512, 512), 512)
-
     def out_ready(s, carry):
         target = owner(s)
         dws[target, 0] = gacc[:, lanes_of(target)].astype(BF)
@@ -958,31 +958,38 @@
         return carry
 
     lax.fori_loop(0, im, experts_back, 0)
-    reduce_forward(0, first_steps)
-
-    def in_grads(s, carry):
+
+    def in_grads(target):
+        accf[...] = tn(recv[0], slopes[target, 0])
+
+        def more(i, carry):
+            accf[...] += tn(recv[i], slopes[target, i])
+            return carry
+
+        lax.fori_loop(1, im, more, 0)
+        dws[target, 1] = accf[...].astype(BF)
+
+    def end_in_grads(s, carry):
         target = owner(s)
-        gacc[:, 0:512] = tn(recv[0], slopes[target, 0])
-
-        def more(i, carry):
-            gacc[:, 0:512] += tn(recv[i], slopes[target, i])
-            return carry
-
-        lax.fori_loop(1, im, more, 0)
-        dws[target, 1] = gacc[:, 0:512].astype(BF)
-
-        @pl.when(ends & (s < 2))
+        in_grads(target)
+
+        @pl.when(s < 2)
         def _():
             reduce_start(target, 1)
 
         return carry
 
-    lax.fori_loop(0, n_z, in_grads, 0)
+    def inner_in_grads(s, carry):
+        in_grads(jnp.where(s == 0, far_end, jnp.where(s == 1, middle, jnp.where(s == 2, near_end, z))))
+        return carry
+
+    @pl.when(ends)
+    def _():
+        lax.fori_loop(0, n_z, end_in_grads, 0)
 
     gacc[...] = jnp.zeros_like(gacc)
     each(own_mixed, "wait")
     home_sent(xin, mix_ss)
-    reduce_forward(0, second_steps)
 
     def back(i, carry):
         arrive(i, ret, dn_rs)
@@ -1008,12 +1015,12 @@
             grads = ([], [], [])
             for side in range(2):
                 head = pair * 2 + side
-                scores = nt(q2 * masks[side], k2) * 0.125
+                scores = nt(q2 * eighths[side], k2)
                 scores = jnp.where(keys_ok, scores, NEG)
                 prob = jnp.exp(scores - here[:, head : head + 1])
                 dprob = nt(do2 * masks[side], v2)
-                inner = jnp.sum(prob * dprob, axis=-1, keepdims=True)
-                ds = (prob * (dprob - inner)).astype(BF)
+                weighted = jnp.sum(prob * dprob, axis=-1, keepdims=True)
+                ds = (prob * (dprob - weighted)).astype(BF)
                 grads[0].append(nn(ds, k2))
                 grads[1].append(tn(ds, q2))
                 grads[2].append(tn(prob.astype(BF), do2))
@@ -1033,16 +1040,21 @@
 
         @pl.when(i == 0)
         def _():
+            reduce_forward(0, first_steps)
+
+        @pl.when(i == 2)
+        def _():
+            reduce_forward(0, second_steps)
+
+            @pl.when(inner)
+            def _():
+                lax.fori_loop(0, 1, inner_in_grads, 0)
+
             reduce_forward(1, first_steps)
 
-        @pl.when(i == 1)
-        def _():
-            reduce_forward(1, second_steps)
-
         return carry
 
     lax.fori_loop(0, im, back, 0)
-    home_start(xin, gtok, gt_ss, gt_rs, sizes[:1])
     own_gtok = home_own(xin, gtok, loc_sem.at[1])
     each(own_gtok, "start")
 
@@ -1050,6 +1062,11 @@
         csend[q] = gacc[rows_of(2 * q + 1 - core, 64)].astype(BF)
         remote(csend.at[q], crecv.at[q], c_ss.at[q], c_rs.at[q], partner, z).start()
     remote(gvec, cvec, cv_ss.at[0], cv_rs.at[0], partner, z).start()
+
+    @pl.when(inner)
+    def _():
+        lax.fori_loop(1, 3, inner_in_grads, 0)
+
     for q in range(half):
         remote(crecv.at[q], crecv.at[q], c_ss.at[q], c_rs.at[q], me, z).wait_recv()
     for k in range(1, half):
@@ -1061,30 +1078,29 @@
     for k in range(1, half):
         q = lax.rem(chip + k, half)
         remote(hvec.at[chip], hvec.at[chip], hv_ss.at[k], hv_rs.at[chip], q * 2 + core, z).start()
+    reduce_forward(1, second_steps)
+
+    @pl.when(inner)
+    def _():
+        lax.fori_loop(3, n_z, inner_in_grads, 0)
+
     dense = gacc[rows_of(me, 64)] + crecv[chip].astype(F32)
     for k in range(1, half):
         q = lax.rem(chip + k, half)
         remote(hrecv.at[q], hrecv.at[q], h_ss.at[0], h_rs.at[q], me, z).wait_recv()
         dense = dense + hrecv[q].astype(F32)
-    for h in range(2):
-        zsend[h] = dense[h * 32 : h * 32 + 32].astype(BF)
-
-        @pl.when(z == h + 1)
-        def _():
-            zrecv[z] = zsend[h]
-
-        @pl.when(z != h + 1)
-        def _():
-            remote(zsend.at[h], zrecv.at[z], za_ss.at[h], za_rs.at[z], me, h + 1).start()
-
+    gacc[0:64] = dense
     for k in range(1, half):
         q = lax.rem(chip + k, half)
         remote(hvec.at[q], hvec.at[q], hv_ss.at[0], hv_rs.at[q], me, z).wait_recv()
-    zvec[z] = hvec[0] + hvec[1] + hvec[2] + hvec[3]
-
-    @pl.when(z != 1)
+    zvec[0] = hvec[0] + hvec[1] + hvec[2] + hvec[3]
+
+    @pl.when(ends)
     def _():
-        remote(zvec.at[z], zvec.at[z], zv_ss.at[0], zv_rs.at[z], me, 1).start()
+        zsend[...] = gacc[0:64].astype(BF)
+        peer = jnp.where(z == 0, 1, last - 1)
+        remote(zsend, zrecv.at[0], za_ss.at[0], za_rs.at[0], me, peer).start()
+        remote(zvec.at[0], zvec.at[1], zv_ss.at[0], zv_rs.at[1], me, peer).start()
 
     @pl.when(ends)
     def _():
@@ -1092,6 +1108,22 @@
         reduce_start(owner(2), 1)
 
     home_start(xin, gtok, gt_ss, gt_rs, sizes[1:])
+
+    @pl.when(inner)
+    def _():
+        remote(zrecv.at[0], zrecv.at[0], za_ss.at[0], za_rs.at[0], me, z).wait_recv()
+        zsend[...] = (gacc[0:64] + zrecv[0].astype(F32)).astype(BF)
+        remote(zsend, zrecv.at[1], za_ss.at[1], za_rs.at[1], me, middle).start()
+        home_start(xin, gtok, gt_ss, gt_rs, sizes[:1])
+        remote(zvec.at[1], zvec.at[1], zv_ss.at[0], zv_rs.at[1], me, z).wait_recv()
+        zvec[2] = zvec[0] + zvec[1]
+        remote(zvec.at[2], zvec.at[3], zv_ss.at[1], zv_rs.at[3], me, middle).start()
+        remote(zrecv.at[1], zrecv.at[1], za_ss.at[0], za_rs.at[1], me, z).wait_recv()
+        zall[...] = (zsend[...].astype(F32) + zrecv[1].astype(F32)).astype(BF)
+        remote(zall, zall, zb_ss.at[0], zb_rs.at[0], me, near_end).start()
+        remote(zvec.at[3], zvec.at[3], zv_ss.at[0], zv_rs.at[3], me, z).wait_recv()
+        zvec[4] = zvec[2] + zvec[3]
+        remote(zvec.at[4], zvec.at[4], zv_ss.at[2], zv_rs.at[4], me, near_end).start()
 
     final_copies = [
         pltpu.make_async_copy(gacc.at[:, pl.ds(piece * 512, 512)], out, loc_sem.at[2 + piece])
@@ -1116,42 +1148,14 @@
 
         lax.fori_loop(0, 4, finish, 0)
         final_copies[piece].start()
-    for h in range(2):
-
-        @pl.when(z == h + 1)
-        def _():
-            z_arrive(lambda i: zrecv.at[i], za_rs)
-            total = zrecv[0].astype(F32)
-            for k in range(1, n_z):
-                total = total + zrecv[k].astype(F32)
-            zall[h] = total.astype(BF)
-            for k in range(1, n_z):
-                peer = lax.rem(z + k, n_z)
-                remote(zall.at[h], zall.at[h], zb_ss.at[k], zb_rs.at[h], me, peer).start()
-
-    @pl.when(z == 1)
+    @pl.when(ends)
     def _():
-        z_arrive(lambda i: zvec.at[i], zv_rs)
-        gsmall[...] = zvec[0] + zvec[1] + zvec[2] + zvec[3]
-        zvec[n_z] = gsmall[...]
-        for k in range(1, n_z):
-            peer = lax.rem(z + k, n_z)
-            remote(zvec.at[n_z], zvec.at[n_z], zv_ss.at[k], zv_rs.at[n_z], me, peer).start()
-
-    @pl.when(z != 1)
-    def _():
-        remote(zvec.at[n_z], zvec.at[n_z], zv_ss.at[0], zv_rs.at[n_z], me, z).wait_recv()
-        gsmall[...] = zvec[n_z]
-
-    for h in range(2):
-
-        @pl.when(z != h + 1)
-        def _():
-            remote(zall.at[h], zall.at[h], zb_ss.at[0], zb_rs.at[h], me, z).wait_recv()
-
-        piece = zall[h].astype(F32)
-        gqkv[h * 32 : h * 32 + 32] = piece[:, 0:1536]
-        gwo[h * 32 : h * 32 + 32] = piece[:, 1536:2048]
+        remote(zvec.at[4], zvec.at[4], zv_ss.at[0], zv_rs.at[4], me, z).wait_recv()
+        remote(zall, zall, zb_ss.at[0], zb_rs.at[0], me, z).wait_recv()
+
+    gsmall[...] = zvec[4]
+    gqkv[...] = zall[:, 0:1536].astype(F32)
+    gwo[...] = zall[:, 1536:2048].astype(F32)
     each(own_gtok, "wait")
     home_arrive(gtok, gt_rs)
     home_arrive(mixed, mix_rs)
@@ -1162,23 +1166,17 @@
     hosts_sent(rin, rts_ss)
     hosts_sent(tin, tgt_ss)
     home_sent(xin, gt_ss)
-    for h in range(2):
-
-        @pl.when(z != h + 1)
-        def _():
-            remote(zsend.at[h], zsend.at[h], za_ss.at[h], loc_sem.at[8], me, z).wait_send()
-
-        @pl.when(z == h + 1)
-        def _():
-            z_sent(lambda peer: zall.at[0], zb_ss)
-
-    @pl.when(z == 1)
+    @pl.when(ends)
     def _():
-        z_sent(lambda peer: zvec.at[0], zv_ss)
-
-    @pl.when(z != 1)
+        remote(zsend, zsend, za_ss.at[0], loc_sem.at[8], me, z).wait_send()
+        remote(zvec.at[0], zvec.at[0], zv_ss.at[0], loc_sem.at[8], me, z).wait_send()
+
+    @pl.when(inner)
     def _():
-        remote(zvec.at[0], zvec.at[0], zv_ss.at[0], loc_sem.at[8], me, z).wait_send()
+        remote(zsend, zsend, za_ss.at[1], loc_sem.at[8], me, z).wait_send()
+        remote(zall, zall, zb_ss.at[0], loc_sem.at[8], me, z).wait_send()
+        for k in (1, 2):
+            remote(zvec.at[0], zvec.at[0], zv_ss.at[k], loc_sem.at[8], me, z).wait_send()
 
 
     def rows_sent(i, carry):
@@ -1215,9 +1213,12 @@
     outs[1][...] = gtok[...].astype(F32)
     for source, target in ((gqkv, outs[2]), (gwo, outs[3]), (gin, outs[4]), (gout, outs[5])):
         target[...] = source[...]
+
     lanes = gsmall[:, pl.ds(pl.multiple_of((me // 2) * 128, 128), 128)]
     lanes = jnp.where(lax.rem(me, 2) == 1, pltpu.roll(lanes, 64, 1), lanes)
-    outs[6][...] = lanes[:, 0:64]
+    for row in range(4):
+        outs[6 + row][...] = lanes[row, 0:64]
+    outs[10][...] = lanes[8:16, 0:64]
 
 
 def whole_images(
@@ -1269,17 +1270,17 @@
             vm((n_z, 512, 512), BF), vm((n_z, 512, 512), BF), vm((im, 512, 512), BF), vm((im, 512, 512), BF),
             vm((n_z, im, 512, 512), BF), vm((n_z, im, 512, 512), BF), vm((im, 512, 512), BF),
             vm((im, 512, 512), BF), vm((im, sp, width), F32), vm((n_z, 2, 512, 512), BF), vm((5, 2, 512, 512), BF),
-            vm((width, 2048), F32), vm((16, width), F32), vm((half, 64, 2048), BF), vm((half, 64, 2048), BF),
+            vm((width, 2048), F32), vm((512, 512), F32), vm((16, width), F32), vm((half, 64, 2048), BF), vm((half, 64, 2048), BF),
             vm((16, width), F32), vm((half, 64, 2048), BF), vm((half, 16, width), F32),
-            vm((2, 32, 2048), BF), vm((n_z, 32, 2048), BF), vm((2, 32, 2048), BF), vm((n_z + 1, 16, width), F32),
+            vm((64, 2048), BF), vm((2, 64, 2048), BF), vm((64, 2048), BF), vm((5, 16, width), F32),
             dma((9,)), dma((n_z,)), dma((n_z,)), dma((n_z,)), dma((n_z,)), dma((n_z,)), dma((n_z,)),
             dma((3, half)), dma((3, n_dp)), dma((3, half)), dma((2, n_z)), dma((n_z,)), dma((2, n_z)), dma((n_z,)),
             dma((im, n_dp)), dma((im, n_dp)), dma((im, n_dp)), dma((im, n_dp)), dma((im, n_dp)), dma((im, n_dp)),
             dma((im, n_dp)), dma((im, n_dp)),
             dma((n_z,)), dma((n_z,)), dma((n_z,)), dma((n_z,)),
             dma((n_z, 2)), dma((5, 2)), dma((half,)), dma((half,)), dma((1,)), dma((1,)),
-            dma((half,)), dma((half,)), dma((half,)), dma((half,)), dma((2,)), dma((n_z,)), dma((n_z,)), dma((2,)),
-            dma((n_z,)), dma((n_z + 1,)),
+            dma((half,)), dma((half,)), dma((half,)), dma((half,)), dma((2,)), dma((2,)), dma((1,)), dma((1,)),
+            dma((3,)), dma((5,)),
         ],
         compiler_params=pltpu.CompilerParams(
             collective_id=1, has_side_effects=True, vmem_limit_bytes=VMEM_LIMIT
@@ -1287,7 +1288,7 @@
         name="block",
     )(tokens, targets, lines, w_qkv, w_out, vec, expert_in[0], expert_out[0])
     whole = pl.BlockSpec(memory_space=pltpu.VMEM)
-    mixed, gtok, gqkv, gwo, gin, gout, part = pl.pallas_call(
+    mixed, gtok, gqkv, gwo, gin, gout, g1, b1, g2, b2, grouter = pl.pallas_call(
         finish_kernel,
         out_shape=[
             jax.ShapeDtypeStruct((image_count, block, width), BF),
@@ -1296,25 +1297,14 @@
             jax.ShapeDtypeStruct((64, width), F32),
             jax.ShapeDtypeStruct((512, 512), F32),
             jax.ShapeDtypeStruct((512, 512), F32),
-            jax.ShapeDtypeStruct((16, 64), F32),
-        ],
+        ]
+        + [jax.ShapeDtypeStruct((64,), F32)] * 4
+        + [jax.ShapeDtypeStruct((8, 64), F32)],
         in_specs=[whole] * 7,
-        out_specs=[whole] * 7,
+        out_specs=[whole] * 11,
         name="finish",
     )(mixed, gtok, gqkv, gwo, gsmall, gin, gout)
-    return (
-        mixed,
-        gtok,
-        part[0],
-        part[1],
-        gqkv,
-        gwo,
-        part[2],
-        part[3],
-        jnp.transpose(part[8:16]),
-        gin[None],
-        gout[None],
-    )
+    return (mixed, gtok, g1, b1, gqkv, gwo, g2, b2, jnp.transpose(grouter), gin[None], gout[None])
 
 
 def fits(tokens, w_qkv, w_router, expert_in):

time: 225 us -> 212 us (0.942)
  Pallas kernels: 218 us -> 207 us
  local copies, waits for them, and re-layouts: 4.23 us -> 1.61 us
    pallas_call x1, Pallas kernels: 213 us -> 203 us  [whole_images(): pl.pallas_call(functools.partial(block_kernel, dims), out_shape=[jax.Shap...]
where the time goes in v3:
time: 212 us; the launch traced here: 211 us
  Pallas kernels  207 us (98%)
    pallas_call x1, Pallas kernels, whole_images(): pl.pallas_call(functools.partial(block_kernel, dims), out_shape=[jax.Shap...  203 us
    pallas_call x1, Pallas kernels, whole_images(): pl.pallas_call(finish_kernel, out_shape=[jax.ShapeDtypeStruct((image_coun...  4.45 us

profile of v3, /device:TPU:0, one launch (start us, length us, event | category | flops | bytes accessed | tf_op | source)
XLA Modules:
  0.0 211.0 jit_solution(9489304252362474292)
XLA Ops:
  0.7 1.4 concatenate.7
  2.1 0.7 select_bitcast_fusion
  2.8 0.2 dynamic_update_slice.3.vec
  3.0 0.0 copy-start
  3.0 0.7 pad_add_fusion.rts
  3.7 0.0 copy-done
  3.7 202.8 %block.1 = (bf16[12,50,512]{2,1,0:T(8,128)(2,1)}, bf16[12,50,512]{2,1,0:T(8,128)(2,1)}, f32[64,1536]{1,0:T(8,128)}, f32[64,512]{1,0:T(8,128)}, f32[16,512]{1,0:T...) custom-call(bf16[12,50,512]{2,1,0:T(8,128)(2,1)} %tok.1, bf16[12,50,512]{2,1,0:T(8,128)(2,1)} %tgt.1, ...), custom_call_target="tpu_custom_call" | custom-call | tf_op jit(solution)/shard_map/block/pallas_call | solution.py:1252
  206.5 4.4 %finish.1 = (bf16[12,50,512]{2,1,0:T(8,128)(2,1)}, f32[12,50,512]{2,1,0:T(8,128)}, f32[64,1536]{1,0:T(8,128)}, f32[64,512]{1,0:T(8,128)}, f32[512,512]{1,0:T(8,1...) custom-call(bf16[12,50,512]{2,1,0:T(8,128)(2,1)} %get-tuple-element., ...), custom_call_target="tpu_custom_call" | custom-call | tf_op jit(solution)/shard_map/finish/pallas_call | solution.py:1291
  (4 shorter events, 0.0 us)
Async XLA Ops:
  3.0 0.7 copy-start

commit v4 on v3

--- a/solution.py
+++ b/solution.py
@@ -890,6 +890,14 @@
 
     lax.fori_loop(0, im, gates_back, 0)
 
+    def turn(i, carry):
+        recv[i] = jnp.transpose(recv[i])
+        for shard in range(n_z):
+            acts[shard, i] = jnp.transpose(acts[shard, i])
+        return carry
+
+    lax.fori_loop(0, im, turn, 0)
+
     def reduce_start(target, piece):
         peer = jnp.where(z == 0, 1, last - 1)
         slot = jnp.where(target == peer, 0, jnp.where(target == far_end, 2, 1))
@@ -941,7 +949,7 @@
         arrive(i, drows, du_rs)
         du = drows[i]
         for target in range(n_z):
-            gacc[:, target * 512 : target * 512 + 512] += tn(acts[target, i], du)
+            gacc[:, target * 512 : target * 512 + 512] += nn(acts[target, i], du)
 
         @pl.when(i == im - 1)
         def _():
@@ -960,10 +968,10 @@
     lax.fori_loop(0, im, experts_back, 0)
 
     def in_grads(target):
-        accf[...] = tn(recv[0], slopes[target, 0])
+        accf[...] = nn(recv[0], slopes[target, 0])
 
         def more(i, carry):
-            accf[...] += tn(recv[i], slopes[target, i])
+            accf[...] += nn(recv[i], slopes[target, i])
             return carry
 
         lax.fori_loop(1, im, more, 0)
@@ -990,6 +998,8 @@
     gacc[...] = jnp.zeros_like(gacc)
     each(own_mixed, "wait")
     home_sent(xin, mix_ss)
+
+    reduce_forward(0, first_steps)
 
     def back(i, carry):
         arrive(i, ret, dn_rs)
@@ -1038,13 +1048,12 @@
         for b in range(n_z):
             xin[b, i] = dx[b * BP : b * BP + block]
 
-        @pl.when(i == 0)
+        @pl.when(i == 1)
         def _():
-            reduce_forward(0, first_steps)
+            reduce_forward(0, second_steps)
 
         @pl.when(i == 2)
         def _():
-            reduce_forward(0, second_steps)
 
             @pl.when(inner)
             def _():

time: 212 us -> 210 us (level)
  no operation moved by 1% of the time
where the time goes in v4:
time: 210 us
  Pallas kernels  206 us (98%)
    pallas_call x1, Pallas kernels, whole_images(): pl.pallas_call(functools.partial(block_kernel, dims), out_shape=[jax.Shap...  201 us
    pallas_call x1, Pallas kernels, whole_images(): pl.pallas_call(finish_kernel, out_shape=[jax.ShapeDtypeStruct((image_coun...  4.45 us

profile of v4, /device:TPU:0, one launch (start us, length us, event | category | flops | bytes accessed | tf_op | source)
XLA Modules:
  0.0 209.5 jit_solution(11312301436702187440)
XLA Ops:
  0.7 1.4 concatenate.7
  2.1 0.7 select_bitcast_fusion
  2.8 0.2 dynamic_update_slice.3.vec
  3.0 0.0 copy-start
  3.0 0.7 pad_add_fusion.rts
  3.7 0.0 copy-done
  3.7 201.3 %block.1 = (bf16[12,50,512]{2,1,0:T(8,128)(2,1)}, bf16[12,50,512]{2,1,0:T(8,128)(2,1)}, f32[64,1536]{1,0:T(8,128)}, f32[64,512]{1,0:T(8,128)}, f32[16,512]{1,0:T...) custom-call(bf16[12,50,512]{2,1,0:T(8,128)(2,1)} %tok.1, bf16[12,50,512]{2,1,0:T(8,128)(2,1)} %tgt.1, ...), custom_call_target="tpu_custom_call" | custom-call | tf_op jit(solution)/shard_map/block/pallas_call | solution.py:1261
  205.0 4.4 %finish.1 = (bf16[12,50,512]{2,1,0:T(8,128)(2,1)}, f32[12,50,512]{2,1,0:T(8,128)}, f32[64,1536]{1,0:T(8,128)}, f32[64,512]{1,0:T(8,128)}, f32[512,512]{1,0:T(8,1...) custom-call(bf16[12,50,512]{2,1,0:T(8,128)(2,1)} %get-tuple-element., ...), custom_call_target="tpu_custom_call" | custom-call | tf_op jit(solution)/shard_map/finish/pallas_call | solution.py:1300
  (4 shorter events, 0.0 us)
Async XLA Ops:
  3.0 0.7 copy-start

commit v5 on v4

--- a/solution.py
+++ b/solution.py
@@ -1064,6 +1064,25 @@
         return carry
 
     lax.fori_loop(0, im, back, 0)
+
+    def inner_tokens(near):
+        @pl.when(inner)
+        def _():
+            for k in range(1, n_z):
+                peer = lax.rem(z + k, n_z)
+
+                @pl.when((peer == near_end) if near else (peer != near_end))
+                def _():
+                    remote(
+                        xin.at[peer, pl.ds(0, counts[1])],
+                        gtok.at[pl.ds(first, counts[1])],
+                        gt_ss.at[k],
+                        gt_rs.at[z],
+                        me,
+                        peer,
+                    ).start()
+
+    inner_tokens(True)
     own_gtok = home_own(xin, gtok, loc_sem.at[1])
     each(own_gtok, "start")
 
@@ -1123,7 +1142,6 @@
         remote(zrecv.at[0], zrecv.at[0], za_ss.at[0], za_rs.at[0], me, z).wait_recv()
         zsend[...] = (gacc[0:64] + zrecv[0].astype(F32)).astype(BF)
         remote(zsend, zrecv.at[1], za_ss.at[1], za_rs.at[1], me, middle).start()
-        home_start(xin, gtok, gt_ss, gt_rs, sizes[:1])
         remote(zvec.at[1], zvec.at[1], zv_ss.at[0], zv_rs.at[1], me, z).wait_recv()
         zvec[2] = zvec[0] + zvec[1]
         remote(zvec.at[2], zvec.at[3], zv_ss.at[1], zv_rs.at[3], me, middle).start()
@@ -1133,6 +1151,7 @@
         remote(zvec.at[3], zvec.at[3], zv_ss.at[0], zv_rs.at[3], me, z).wait_recv()
         zvec[4] = zvec[2] + zvec[3]
         remote(zvec.at[4], zvec.at[4], zv_ss.at[2], zv_rs.at[4], me, near_end).start()
+        inner_tokens(False)
 
     final_copies = [
         pltpu.make_async_copy(gacc.at[:, pl.ds(piece * 512, 512)], out, loc_sem.at[2 + piece])

time: 210 us -> 207 us (0.986)
  Pallas kernels: 206 us -> 202 us
    pallas_call x1, Pallas kernels: 201 us -> 198 us  [whole_images(): pl.pallas_call(functools.partial(block_kernel, dims), out_shape=[jax.Shap...]
where the time goes in v5:
time: 207 us; the launch traced here: 206 us
  Pallas kernels  202 us (98%)
    pallas_call x1, Pallas kernels, whole_images(): pl.pallas_call(functools.partial(block_kernel, dims), out_shape=[jax.Shap...  198 us
    pallas_call x1, Pallas kernels, whole_images(): pl.pallas_call(finish_kernel, out_shape=[jax.ShapeDtypeStruct((image_coun...  4.45 us

profile of v5, /device:TPU:0, one launch (start us, length us, event | category | flops | bytes accessed | tf_op | source)
XLA Modules:
  0.0 205.9 jit_solution(9772802922126987163)
XLA Ops:
  0.7 1.4 concatenate.7
  2.1 0.7 select_bitcast_fusion
  2.8 0.2 dynamic_update_slice.3.vec
  3.0 0.0 copy-start
  3.0 0.7 pad_add_fusion.rts
  3.7 0.0 copy-done
  3.7 197.6 %block.1 = (bf16[12,50,512]{2,1,0:T(8,128)(2,1)}, bf16[12,50,512]{2,1,0:T(8,128)(2,1)}, f32[64,1536]{1,0:T(8,128)}, f32[64,512]{1,0:T(8,128)}, f32[16,512]{1,0:T...) custom-call(bf16[12,50,512]{2,1,0:T(8,128)(2,1)} %tok.1, bf16[12,50,512]{2,1,0:T(8,128)(2,1)} %tgt.1, ...), custom_call_target="tpu_custom_call" | custom-call | tf_op jit(solution)/shard_map/block/pallas_call | solution.py:1280
  201.4 4.4 %finish.1 = (bf16[12,50,512]{2,1,0:T(8,128)(2,1)}, f32[12,50,512]{2,1,0:T(8,128)}, f32[64,1536]{1,0:T(8,128)}, f32[64,512]{1,0:T(8,128)}, f32[512,512]{1,0:T(8,1...) custom-call(bf16[12,50,512]{2,1,0:T(8,128)(2,1)} %get-tuple-element., ...), custom_call_target="tpu_custom_call" | custom-call | tf_op jit(solution)/shard_map/finish/pallas_call | solution.py:1319
  (4 shorter events, 0.0 us)
Async XLA Ops:
  3.0 0.7 copy-start

commit v6 on v5

--- a/solution.py
+++ b/solution.py
@@ -833,7 +833,7 @@
     gacc[...] = jnp.zeros_like(gacc)
 
     def mix(i, carry):
-        @pl.when(i == 1)
+        @pl.when(i == 0)
         def _():
             hosts_start(tgt, tin, tgt_ss, tgt_rs, (0, last), inner)
 

time: 207 us -> 208 us (level)
  no operation moved by 1% of the time
where the time goes in v6:
time: 208 us; the launch traced here: 207 us
  Pallas kernels  203 us (98%)
    pallas_call x1, Pallas kernels, whole_images(): pl.pallas_call(functools.partial(block_kernel, dims), out_shape=[jax.Shap...  199 us
    pallas_call x1, Pallas kernels, whole_images(): pl.pallas_call(finish_kernel, out_shape=[jax.ShapeDtypeStruct((image_coun...  4.45 us

profile of v6, /device:TPU:0, one launch (start us, length us, event | category | flops | bytes accessed | tf_op | source)
XLA Modules:
  0.0 207.2 jit_solution(14619003507580220409)
XLA Ops:
  0.7 1.4 concatenate.7
  2.1 0.7 select_bitcast_fusion
  2.8 0.2 dynamic_update_slice.3.vec
  3.0 0.0 copy-start
  3.0 0.7 pad_add_fusion.rts
  3.7 0.0 copy-done
  3.7 198.9 %block.1 = (bf16[12,50,512]{2,1,0:T(8,128)(2,1)}, bf16[12,50,512]{2,1,0:T(8,128)(2,1)}, f32[64,1536]{1,0:T(8,128)}, f32[64,512]{1,0:T(8,128)}, f32[16,512]{1,0:T...) custom-call(bf16[12,50,512]{2,1,0:T(8,128)(2,1)} %tok.1, bf16[12,50,512]{2,1,0:T(8,128)(2,1)} %tgt.1, ...), custom_call_target="tpu_custom_call" | custom-call | tf_op jit(solution)/shard_map/block/pallas_call | solution.py:1280
  202.7 4.4 %finish.1 = (bf16[12,50,512]{2,1,0:T(8,128)(2,1)}, f32[12,50,512]{2,1,0:T(8,128)}, f32[64,1536]{1,0:T(8,128)}, f32[64,512]{1,0:T(8,128)}, f32[512,512]{1,0:T(8,1...) custom-call(bf16[12,50,512]{2,1,0:T(8,128)(2,1)} %get-tuple-element., ...), custom_call_target="tpu_custom_call" | custom-call | tf_op jit(solution)/shard_map/finish/pallas_call | solution.py:1319
  (4 shorter events, 0.0 us)
Async XLA Ops:
  3.0 0.7 copy-start
